TPU v7x, 32 devices: a whole 2x2x4 slice. The times are simulated.
32 devices in a mesh: groups: 2 (over y), tile: 4 (over z), depth: 4 (over x, core).
Axes of the slice: x: 2, y: 2, z: 4, core: 2. Of those that a mesh axis runs over, the one named last changes fastest.
Arguments:
- volume: bfloat16 [64, 64, 32, 128], P(None, ('groups', 'depth'), 'tile'), parts along dimension 1, may hold values from -6 to 6
- first_kernel: bfloat16 [27, 64, 64], replicated, may hold values from -0.15625 to 0.15625
- first_bias: float32 [64], replicated, may hold values from -3 to 3
- second_kernel: bfloat16 [27, 64, 64], replicated, may hold values from -0.15625 to 0.15625
- second_bias: float32 [64], replicated, may hold values from -3 to 3
- density_weight: bfloat16 [64], replicated, may hold values from -0.75 to 0.75
Outputs:
- image: float32 [64, 64, 128], P('depth', ('groups', 'tile')), parts along dimension 1
There are 2 independent parts, one for each index of `groups`. A program takes and returns all parts, laid end to end along the dimension named above; an argument that names none is the same for every part. Nothing has to cross between parts.
All inputs are finite; a program needn't handle non-finite values.
Results may differ from a plain program's by a relative error of at most 0.0015.
Values may be sent and summed in bfloat16 or wider, within the bound.
No kernel may reach another device: no remote copies, remote signals or barrier semaphores. Data moves between devices by JAX's collectives and lax.ppermute only.
A program may use at most 192 MiB of HBM per device.

v0:
```python
import jax
import jax.numpy as jnp
from jax import lax
from jax.sharding import PartitionSpec as P


def extended(block, sides, width):
    for axis, dim in sides:
        count = lax.axis_size(axis)
        forward = [(i, i + 1) for i in range(count - 1)]
        backward = [(target, source) for source, target in forward]
        low = lax.ppermute(
            lax.slice_in_dim(block, block.shape[dim] - width, None, axis=dim), axis, forward
        )
        high = lax.ppermute(lax.slice_in_dim(block, 0, width, axis=dim), axis, backward)
        block = jnp.concatenate([low, block, high], axis=dim)
    return block


def convolve(padded, kernel, bias, spacing, depth_len, rows_len):
    widened = jnp.pad(padded, ((0, 0), (0, 0), (0, 0), (spacing, spacing)))
    cols_len = widened.shape[3] - 2 * spacing
    chans_in = kernel.shape[2]
    chans_out = kernel.shape[1]
    total = jnp.zeros((chans_out, depth_len, rows_len, cols_len), jnp.float32)
    for shift_z in range(3):
        pieces = []
        for shift_x in range(3):
            for shift_y in range(3):
                pieces.append(
                    widened[
                        :,
                        shift_z * spacing : shift_z * spacing + depth_len,
                        shift_x * spacing : shift_x * spacing + rows_len,
                        shift_y * spacing : shift_y * spacing + cols_len,
                    ]
                )
        stacked = jnp.stack(pieces, axis=0).reshape(9 * chans_in, depth_len, rows_len, cols_len)
        taps_flat = (
            kernel[9 * shift_z : 9 * shift_z + 9]
            .transpose(1, 0, 2)
            .reshape(chans_out, 9 * chans_in)
        )
        total = total + jnp.einsum(
            "oc,czxy->ozxy", taps_flat, stacked, preferred_element_type=jnp.float32
        )
    return jax.nn.silu(total + bias[:, None, None, None])


def body(volume, first_kernel, first_bias, second_kernel, second_bias, density_weight):
    chans, slab_len, rows_len, cols_len = volume.shape
    depth_count = lax.axis_size("depth")
    padded = extended(volume, (("tile", 2), ("depth", 1)), 1)
    hidden = convolve(padded, first_kernel, first_bias, 1, slab_len, rows_len).astype(jnp.bfloat16)
    padded_hidden = extended(hidden, (("tile", 2), ("depth", 1)), 2)
    features = convolve(padded_hidden, second_kernel, second_bias, 2, slab_len, rows_len).astype(
        jnp.bfloat16
    )
    logits = jnp.einsum("c,czxy->zxy", density_weight, features, preferred_element_type=jnp.float32)
    tau = jax.nn.softplus(logits) * (2.0 / (slab_len * depth_count))
    inner = jnp.cumsum(tau, axis=0) - tau
    ray_weight = (jnp.exp(-inner) * -jnp.expm1(-tau)).astype(jnp.bfloat16)
    slab_image = jnp.einsum(
        "zxy,czxy->cxy", ray_weight, features, preferred_element_type=jnp.float32
    )
    slab_depth = jnp.sum(tau, axis=0)
    depths_all = lax.all_gather(slab_depth[None], "depth", axis=0, tiled=True)
    prior_all = jnp.cumsum(depths_all, axis=0) - depths_all
    pieces = lax.all_to_all(slab_image[None], "depth", split_axis=1, concat_axis=0, tiled=True)
    return jnp.sum(jnp.exp(-prior_all)[:, None] * pieces, axis=0)


def solution(mesh):
    placed = (P(None, ("groups", "depth"), "tile", None), P(), P(), P(), P(), P())
    return jax.shard_map(
        body,
        mesh=mesh,
        in_specs=placed,
        out_specs=P("depth", ("groups", "tile"), None),
        check_vma=False,
    )
```

profile of v0, /device:TPU:0, one launch (start us, length us, event | category | flops | bytes accessed | tf_op | source)
XLA Modules:
  0.0 107.5 jit_solution(16163670488497147109)
XLA Ops:
  0.0 1.9 %copy.45 = bf16[64,8,8,128]{3,0,2,1:T(8,128)(2,1)S(1)} copy(bf16[64,8,8,128]{3,2,1,0:T(8,128)(2,1)} %param.6) | data formatting | bytes 2097152 | tf_op args[0]
  1.9 5.0 %collective-permute-start = (bf16[64,8,1,128]{3,0,2,1:T(8,128)(2,1)S(1)}, bf16[64,8,1,128]{3,0,2,1:T(8,128)(2,1)S(1)}, u32[]{:S(2)}, u32[]{:S(2)}) collective-permute-start(bf16[64,8,1,128]{3,0,2,1:T(8,128)(2,1)S(1)} %get-tuple-element.41), channel_id=1, source_target_pairs={{0,4},{4,8},{8,12},{1,5},{5,9},{9,13},{2,6},{6,10},{10,14},{3,7},{... | collective-permute-start | bytes 393224 | tf_op jit(solution)/shard_map/ppermute | solution.py:12
  6.9 1.3 %collective-permute-start.1 = (bf16[64,8,1,128]{3,0,2,1:T(8,128)(2,1)S(1)}, bf16[64,8,1,128]{3,0,2,1:T(8,128)(2,1)S(1)}, u32[]{:S(2)}, u32[]{:S(2)}) collective-permute-start(bf16[64,8,1,128]{3,0,2,1:T(8,128)(2,1)S(1)} %get-tuple-element.40), channel_id=1, source_target_pairs={{4,0},{8,4},{12,8},{5,1},{9,5},{13,9},{6,2},{10,6},{14,10},{7,3},{... | collective-permute-start | bytes 393224 | tf_op jit(solution)/shard_map/ppermute | solution.py:15
  8.2 1.4 %collective-permute-done = bf16[64,8,1,128]{3,0,2,1:T(8,128)(2,1)S(1)} collective-permute-done((bf16[64,8,1,128]{3,0,2,1:T(8,128)(2,1)S(1)}, bf16[64,8,1,128]{3,0,2,1:T(8,128)(2,1)S(1)}, u32[]{:S(2)}, u32[]{:S(2)}) %collective-permute-start) | collective-permute-done | bytes 131104 | tf_op jit(solution)/shard_map/ppermute | solution.py:12
  9.7 2.0 %constant_dynamic-update-slice_fusion.1 = bf16[64,8,10,128]{3,0,2,1:T(8,128)(2,1)S(1)} fusion(bf16[64,8,10,128]{3,0,2,1:T(8,128)(2,1)S(1)} %constant_dynamic-update-slice_fusion.2, bf16[64,8,8,128]{3,2,1,0:T(8,128)(2,1)} %param.6), kind=kLoop, calls=%fused_computation.206 | loop fusion | bytes 2097152
  11.6 2.1 %collective-permute-done.1 = bf16[64,8,1,128]{3,0,2,1:T(8,128)(2,1)S(1)} collective-permute-done((bf16[64,8,1,128]{3,0,2,1:T(8,128)(2,1)S(1)}, bf16[64,8,1,128]{3,0,2,1:T(8,128)(2,1)S(1)}, u32[]{:S(2)}, u32[]{:S(2)}) %collective-permute-start.1) | collective-permute-done | bytes 131104 | tf_op jit(solution)/shard_map/ppermute | solution.py:15
  13.8 1.3 %collective-permute-start.2 = (bf16[64,1,10,128]{3,0,2,1:T(8,128)(2,1)S(1)}, bf16[64,1,10,128]{3,0,2,1:T(8,128)(2,1)S(1)}, u32[]{:S(2)}, u32[]{:S(2)}) collective-permute-start(bf16[64,1,10,128]{3,0,2,1:T(8,128)(2,1)S(1)} %get-tuple-element.36), channel_id=1, source_target_pairs={{0,1},{1,2},{2,3},{4,5},{5,6},{6,7},{8,9},{9,10},{10,11},{12,13},{... | collective-permute-start | bytes 491528 | tf_op jit(solution)/shard_map/ppermute | solution.py:12
  15.1 1.3 %collective-permute-start.3 = (bf16[64,1,10,128]{3,0,2,1:T(8,128)(2,1)S(1)}, bf16[64,1,10,128]{3,0,2,1:T(8,128)(2,1)S(1)}, u32[]{:S(2)}, u32[]{:S(2)}) collective-permute-start(bf16[64,1,10,128]{3,0,2,1:T(8,128)(2,1)S(1)} %get-tuple-element.37), channel_id=1, source_target_pairs={{1,0},{2,1},{3,2},{5,4},{6,5},{7,6},{9,8},{10,9},{11,10},{13,12},{... | collective-permute-start | bytes 491528 | tf_op jit(solution)/shard_map/ppermute | solution.py:15
  16.5 3.7 %collective-permute-done.3 = bf16[64,1,10,128]{3,0,2,1:T(8,128)(2,1)S(1)} collective-permute-done((bf16[64,1,10,128]{3,0,2,1:T(8,128)(2,1)S(1)}, bf16[64,1,10,128]{3,0,2,1:T(8,128)(2,1)S(1)}, u32[]{:S(2)}, u32[]{:S(2)}) %collective-permute-start.3) | collective-permute-done | bytes 163872 | tf_op jit(solution)/shard_map/ppermute | solution.py:15
  20.2 2.5 %fusion.21 = bf16[64,10,10,130]{3,0,2,1:T(8,128)(2,1)S(1)} fusion(bf16[64,1,10,128]{3,0,2,1:T(8,128)(2,1)S(1)} %collective-permute-done.3, bf16[64,8,10,128]{3,0,2,1:T(8,128)(2,1)S(1)} %constant_dynamic-update-slice_fusion, bf16[64,1,10,128]{3,0,2,1:T(8,128)(2,1)S(1)} %collective-permute-done.2), kind=kLoop, calls=%fused_computation.27 | loop fusion | flops 9984000 | bytes 3302400 | tf_op jit(solution)/shard_map/concatenate | solution.py:16
  32.1 1.9 %fusion.33 = f32[8,8,128,64]{2,3,0,1:T(8,128)S(1)} fusion(bf16[9,64,8,8,128]{4,1,3,2,0:T(8,128)(2,1)S(1)} %get-tuple-element.22, bf16[27,64,64]{2,1,0:T(8,128)(2,1)S(1)} %copy-done.3), kind=kOutput, calls=%fused_computation.53 | convolution fusion | flops 603979776 | bytes 11681792 | tf_op jit(solution)/shard_map/oc,czxy->ozxy/dot_general | solution.py:44
  34.0 1.9 %fusion.36 = f32[8,8,128,64]{2,3,0,1:T(8,128)S(1)} fusion(bf16[9,64,8,8,128]{4,1,3,2,0:T(8,128)(2,1)S(1)} %fusion.96, bf16[27,64,64]{2,1,0:T(8,128)(2,1)S(1)} %copy-done.3), kind=kOutput, calls=%fused_computation.54 | convolution fusion | flops 603979776 | bytes 11681792 | tf_op jit(solution)/shard_map/oc,czxy->ozxy/dot_general | solution.py:44
  36.0 2.3 %fusion.31 = bf16[64,8,8,128]{3,0,2,1:T(8,128)(2,1)S(1)} fusion(f32[8,8,128,64]{2,3,0,1:T(8,128)S(1)} %fusion.36, f32[8,8,128,64]{2,3,0,1:T(8,128)S(1)} %fusion.33, bf16[9,64,8,8,128]{4,1,0,3,2:T(8,128)(2,1)S(1)} %fusion.114, f32[64]{0:T(128)S(1)} %copy-done.5, bf16[27,64,64]{2,1,0:T(8,128)(2,1)S(1)} %copy-done.3), kind=kOutput, calls=%fused_computation.45 | convolution fusion | flops 608174080 | bytes 14828032 | tf_op jit(solution)/shard_map/oc,czxy->ozxy/dot_general | solution.py:44
  38.3 3.5 %collective-permute-start.4 = (bf16[64,8,2,128]{3,0,2,1:T(8,128)(2,1)S(1)}, bf16[64,8,2,128]{3,0,2,1:T(8,128)(2,1)S(1)}, u32[]{:S(2)}, u32[]{:S(2)}) collective-permute-start(bf16[64,8,2,128]{3,0,2,1:T(8,128)(2,1)S(1)} %get-tuple-element.38), channel_id=1, source_target_pairs={{0,4},{4,8},{8,12},{1,5},{5,9},{9,13},{2,6},{6,10},{10,14},{3,7},{... | collective-permute-start | bytes 786440 | tf_op jit(solution)/shard_map/ppermute | solution.py:12
  41.9 1.3 %collective-permute-start.5 = (bf16[64,8,2,128]{3,0,2,1:T(8,128)(2,1)S(1)}, bf16[64,8,2,128]{3,0,2,1:T(8,128)(2,1)S(1)}, u32[]{:S(2)}, u32[]{:S(2)}) collective-permute-start(bf16[64,8,2,128]{3,0,2,1:T(8,128)(2,1)S(1)} %get-tuple-element.39), channel_id=1, source_target_pairs={{4,0},{8,4},{12,8},{5,1},{9,5},{13,9},{6,2},{10,6},{14,10},{7,3},{... | collective-permute-start | bytes 786440 | tf_op jit(solution)/shard_map/ppermute | solution.py:15
  43.2 2.6 %collective-permute-done.4 = bf16[64,8,2,128]{3,0,2,1:T(8,128)(2,1)S(1)} collective-permute-done((bf16[64,8,2,128]{3,0,2,1:T(8,128)(2,1)S(1)}, bf16[64,8,2,128]{3,0,2,1:T(8,128)(2,1)S(1)}, u32[]{:S(2)}, u32[]{:S(2)}) %collective-permute-start.4) | collective-permute-done | bytes 262176 | tf_op jit(solution)/shard_map/ppermute | solution.py:12
  45.7 4.6 %collective-permute-done.5 = bf16[64,8,2,128]{3,0,2,1:T(8,128)(2,1)S(1)} collective-permute-done((bf16[64,8,2,128]{3,0,2,1:T(8,128)(2,1)S(1)}, bf16[64,8,2,128]{3,0,2,1:T(8,128)(2,1)S(1)}, u32[]{:S(2)}, u32[]{:S(2)}) %collective-permute-start.5) | collective-permute-done | bytes 262176 | tf_op jit(solution)/shard_map/ppermute | solution.py:15
  50.5 4.3 %collective-permute-start.6 = (bf16[64,2,12,128]{3,0,2,1:T(8,128)(2,1)S(1)}, bf16[64,2,12,128]{3,0,2,1:T(8,128)(2,1)S(1)}, u32[]{:S(2)}, u32[]{:S(2)}) collective-permute-start(bf16[64,2,12,128]{3,0,2,1:T(8,128)(2,1)S(1)} %get-tuple-element.34), channel_id=1, source_target_pairs={{0,1},{1,2},{2,3},{4,5},{5,6},{6,7},{8,9},{9,10},{10,11},{12,13},{... | collective-permute-start | bytes 1179656 | tf_op jit(solution)/shard_map/ppermute | solution.py:12
  54.8 1.3 %collective-permute-start.7 = (bf16[64,2,12,128]{3,0,2,1:T(8,128)(2,1)S(1)}, bf16[64,2,12,128]{3,0,2,1:T(8,128)(2,1)S(1)}, u32[]{:S(2)}, u32[]{:S(2)}) collective-permute-start(bf16[64,2,12,128]{3,0,2,1:T(8,128)(2,1)S(1)} %get-tuple-element.35), channel_id=1, source_target_pairs={{1,0},{2,1},{3,2},{5,4},{6,5},{7,6},{9,8},{10,9},{11,10},{13,12},{... | collective-permute-start | bytes 1179656 | tf_op jit(solution)/shard_map/ppermute | solution.py:15
  56.1 2.8 %collective-permute-done.7 = bf16[64,2,12,128]{3,0,2,1:T(8,128)(2,1)S(1)} collective-permute-done((bf16[64,2,12,128]{3,0,2,1:T(8,128)(2,1)S(1)}, bf16[64,2,12,128]{3,0,2,1:T(8,128)(2,1)S(1)}, u32[]{:S(2)}, u32[]{:S(2)}) %collective-permute-start.7) | collective-permute-done | bytes 393248 | tf_op jit(solution)/shard_map/ppermute | solution.py:15
  58.9 4.2 %select_maximum_fusion = bf16[64,12,12,132]{3,0,2,1:T(8,128)(2,1)S(1)} fusion(bf16[64,2,12,128]{3,0,2,1:T(8,128)(2,1)S(1)} %collective-permute-done.7, bf16[64,2,12,128]{3,0,2,1:T(8,128)(2,1)S(1)} %collective-permute-done.6, bf16[64,8,2,128]{3,0,2,1:T(8,128)(2,1)S(1)} %collective-permute-done.5, bf16[64,8,8,128]{3,0,2,1:T(8,128)(2,1)S(1)} %fusion.31, ...), kind=kLoop, calls=%fused_computation.16 | loop fusion | flops 21897216 | bytes 4792320 | tf_op jit(solution)/shard_map/concatenate | solution.py:16
  64.7 2.2 %fusion.93 = (bf16[9,64,8,8,128]{4,1,3,2,0:T(8,128)(2,1)S(1)}, bf16[9,64,8,8,128]{4,1,3,2,0:T(8,128)(2,1)}, bf16[9,64,8,8,128]{4,1,3,2,0:T(8,128)(2,1)S(1)}) fusion(bf16[9,64,8,8,128]{4,1,3,2,0:T(8,128)(2,1)S(1)} %get-tuple-element.43, bf16[64,12,12,132]{3,0,2,1:T(8,128)(2,1)S(1)} %select_maximum_fusion, bf16[9,64,8,8,128]{4,1,3,2,0:T(8,128)(2,1)S(1)} %get-tuple-element.42), kind=kLoop, calls=%fused_computation.133 | loop fusion | bytes 6291456
  68.0 1.9 %fusion.92 = (bf16[9,64,8,8,128]{4,1,3,2,0:T(8,128)(2,1)S(1)}, bf16[9,64,8,8,128]{4,1,3,2,0:T(8,128)(2,1)}, bf16[9,64,8,8,128]{4,1,3,2,0:T(8,128)(2,1)S(1)}) fusion(bf16[9,64,8,8,128]{4,1,3,2,0:T(8,128)(2,1)S(1)} %get-tuple-element.17, bf16[64,12,12,132]{3,0,2,1:T(8,128)(2,1)S(1)} %select_maximum_fusion, bf16[9,64,8,8,128]{4,1,3,2,0:T(8,128)(2,1)} %fusion.75, ...), kind=kLoop, calls=%fused_computation.131 | loop fusion | bytes 6291456
  70.2 2.3 %fusion.90 = (bf16[9,64,8,8,128]{4,1,3,2,0:T(8,128)(2,1)S(1)}, bf16[9,64,8,8,128]{4,1,3,2,0:T(8,128)(2,1)}, bf16[9,64,8,8,128]{4,1,3,2,0:T(8,128)(2,1)S(1)}) fusion(bf16[9,64,8,8,128]{4,1,3,2,0:T(8,128)(2,1)S(1)} %fusion.91, bf16[64,12,12,132]{3,0,2,1:T(8,128)(2,1)S(1)} %select_maximum_fusion, bf16[9,64,8,8,128]{4,1,3,2,0:T(8,128)(2,1)} %get-tuple-element.15, ...), kind=kLoop, calls=%fused_computation.127 | loop fusion | bytes 6291456
  73.5 1.9 %fusion.89 = (bf16[9,64,8,8,128]{4,1,3,2,0:T(8,128)(2,1)S(1)}, bf16[9,64,8,8,128]{4,1,3,2,0:T(8,128)(2,1)}, bf16[9,64,8,8,128]{4,1,3,2,0:T(8,128)(2,1)S(1)}) fusion(bf16[9,64,8,8,128]{4,1,3,2,0:T(8,128)(2,1)S(1)} %get-tuple-element.11, bf16[64,12,12,132]{3,0,2,1:T(8,128)(2,1)S(1)} %select_maximum_fusion, bf16[9,64,8,8,128]{4,1,3,2,0:T(8,128)(2,1)} %fusion.72, ...), kind=kLoop, calls=%fused_computation.125 | loop fusion | bytes 6291456
  75.7 2.2 %fusion.87 = (bf16[9,64,8,8,128]{4,1,3,2,0:T(8,128)(2,1)S(1)}, bf16[9,64,8,8,128]{4,1,3,2,0:T(8,128)(2,1)}, bf16[9,64,8,8,128]{4,1,3,2,0:T(8,128)(2,1)S(1)}) fusion(bf16[9,64,8,8,128]{4,1,3,2,0:T(8,128)(2,1)S(1)} %fusion.88, bf16[64,12,12,132]{3,0,2,1:T(8,128)(2,1)S(1)} %select_maximum_fusion, bf16[9,64,8,8,128]{4,1,3,2,0:T(8,128)(2,1)} %get-tuple-element.9, ...), kind=kLoop, calls=%fused_computation.121 | loop fusion | bytes 6291456 | tf_op jit(solution)/shard_map/stack | solution.py:38
  78.0 1.9 %fusion.39 = f32[8,8,128,64]{2,3,0,1:T(8,128)S(1)} fusion(bf16[9,64,8,8,128]{4,1,3,2,0:T(8,128)(2,1)S(1)} %get-tuple-element.5, bf16[27,64,64]{2,1,0:T(8,128)(2,1)S(1)} %copy-done.4), kind=kOutput, calls=%fused_computation.55 | convolution fusion | flops 603979776 | bytes 11681792 | tf_op jit(solution)/shard_map/oc,czxy->ozxy/dot_general | solution.py:44
  79.9 1.9 %fusion.42 = f32[8,8,128,64]{2,3,0,1:T(8,128)S(1)} fusion(bf16[9,64,8,8,128]{4,1,3,2,0:T(8,128)(2,1)S(1)} %get-tuple-element.7, bf16[27,64,64]{2,1,0:T(8,128)(2,1)S(1)} %copy-done.4), kind=kOutput, calls=%fused_computation.56 | convolution fusion | flops 603979776 | bytes 11681792 | tf_op jit(solution)/shard_map/oc,czxy->ozxy/dot_general | solution.py:44
  83.0 1.5 %fusion.68 = bf16[9,64,8,8,128]{4,1,3,2,0:T(8,128)(2,1)} fusion(bf16[9,64,8,8,128]{4,1,3,2,0:T(8,128)(2,1)} %fusion.69, bf16[64,12,12,132]{3,0,2,1:T(8,128)(2,1)S(1)} %select_maximum_fusion), kind=kLoop, calls=%fused_computation.85 | loop fusion | bytes 2097152 | tf_op jit(solution)/shard_map/stack | solution.py:38
  84.4 5.6 %fusion.45 = f32[8,8,128,64]{2,3,0,1:T(8,128)S(1)} fusion(bf16[9,64,8,8,128]{4,1,3,2,0:T(8,128)(2,1)} %fusion.68, bf16[27,64,64]{2,1,0:T(8,128)(2,1)S(1)} %copy-done.4), kind=kOutput, calls=%fused_computation.57 | convolution fusion | flops 603979776 | bytes 11681792 | tf_op jit(solution)/shard_map/oc,czxy->ozxy/dot_general | solution.py:44
  92.4 7.3 %all-to-all-start = ((f32[1,64,8,128]{3,2,0,1:T(8,128)}), f32[1,64,8,128]{3,2,0,1:T(8,128)S(1)}, u32[]{:S(2)}, u32[]{:S(2)}) async-start(f32[1,64,8,128]{3,2,0,1:T(8,128)} %bitcast.340), calls=%async_computation | async-start | bytes 524288 | tf_op jit(solution)/shard_map/all_to_all | solution.py:69
  99.7 7.0 %all-gather = f32[32,128]{1,0:T(8,128)S(1)} all-gather(f32[8,128]{1,0:T(8,128)S(1)} %fusion.137), channel_id=2, replica_groups=mesh['groups'=2,'tile'=4,'depth'=4] {'depth'}, dimensions={0}, use_global_device_ids=true | all-gather | bytes 20480 | tf_op jit(solution)/shard_map/all_gather | solution.py:67
  (61 shorter events, 17.9 us)
Async XLA Ops:
  0.0 90.9 %copy-start = (bf16[64]{0:T(256)(128)(2,1)S(1)}, bf16[64]{0:T(256)(128)(2,1)}, u32[]{:S(2)}) copy-start(bf16[64]{0:T(256)(128)(2,1)} %param.11) | copy-start | bytes 388
  1.9 7.7 %collective-permute-start = (bf16[64,8,1,128]{3,0,2,1:T(8,128)(2,1)S(1)}, bf16[64,8,1,128]{3,0,2,1:T(8,128)(2,1)S(1)}, u32[]{:S(2)}, u32[]{:S(2)}) collective-permute-start(bf16[64,8,1,128]{3,0,2,1:T(8,128)(2,1)S(1)} %get-tuple-element.41), channel_id=1, source_target_pairs={{0,4},{4,8},{8,12},{1,5},{5,9},{9,13},{2,6},{6,10},{10,14},{3,7},{... | collective-permute-start | bytes 393224 | tf_op jit(solution)/shard_map/ppermute | solution.py:12
  6.9 6.9 %collective-permute-start.1 = (bf16[64,8,1,128]{3,0,2,1:T(8,128)(2,1)S(1)}, bf16[64,8,1,128]{3,0,2,1:T(8,128)(2,1)S(1)}, u32[]{:S(2)}, u32[]{:S(2)}) collective-permute-start(bf16[64,8,1,128]{3,0,2,1:T(8,128)(2,1)S(1)} %get-tuple-element.40), channel_id=1, source_target_pairs={{4,0},{8,4},{12,8},{5,1},{9,5},{13,9},{6,2},{10,6},{14,10},{7,3},{... | collective-permute-start | bytes 393224 | tf_op jit(solution)/shard_map/ppermute | solution.py:15
  13.8 2.6 %collective-permute-start.2 = (bf16[64,1,10,128]{3,0,2,1:T(8,128)(2,1)S(1)}, bf16[64,1,10,128]{3,0,2,1:T(8,128)(2,1)S(1)}, u32[]{:S(2)}, u32[]{:S(2)}) collective-permute-start(bf16[64,1,10,128]{3,0,2,1:T(8,128)(2,1)S(1)} %get-tuple-element.36), channel_id=1, source_target_pairs={{0,1},{1,2},{2,3},{4,5},{5,6},{6,7},{8,9},{9,10},{10,11},{12,13},{... | collective-permute-start | bytes 491528 | tf_op jit(solution)/shard_map/ppermute | solution.py:12
  15.1 5.0 %collective-permute-start.3 = (bf16[64,1,10,128]{3,0,2,1:T(8,128)(2,1)S(1)}, bf16[64,1,10,128]{3,0,2,1:T(8,128)(2,1)S(1)}, u32[]{:S(2)}, u32[]{:S(2)}) collective-permute-start(bf16[64,1,10,128]{3,0,2,1:T(8,128)(2,1)S(1)} %get-tuple-element.37), channel_id=1, source_target_pairs={{1,0},{2,1},{3,2},{5,4},{6,5},{7,6},{9,8},{10,9},{11,10},{13,12},{... | collective-permute-start | bytes 491528 | tf_op jit(solution)/shard_map/ppermute | solution.py:15
  24.9 3.0 %copy-start.1 = (bf16[64,8,8,128]{3,2,1,0:T(8,128)(2,1)S(1)}, bf16[64,8,8,128]{3,2,1,0:T(8,128)(2,1)}, u32[]{:S(2)}) copy-start(bf16[64,8,8,128]{3,2,1,0:T(8,128)(2,1)} %param.6) | copy-start | bytes 3145732
  29.4 2.7 %copy-start.3 = (bf16[27,64,64]{2,1,0:T(8,128)(2,1)S(1)}, bf16[27,64,64]{2,1,0:T(8,128)(2,1)}, u32[]{:S(2)}) copy-start(bf16[27,64,64]{2,1,0:T(8,128)(2,1)} %param.7) | copy-start | bytes 663556
  34.0 2.0 %copy-start.5 = (f32[64]{0:T(128)S(1)}, f32[64]{0:T(128)}, u32[]{:S(2)}) copy-start(f32[64]{0:T(128)} %param.8) | copy-start | bytes 772
  38.3 7.4 %collective-permute-start.4 = (bf16[64,8,2,128]{3,0,2,1:T(8,128)(2,1)S(1)}, bf16[64,8,2,128]{3,0,2,1:T(8,128)(2,1)S(1)}, u32[]{:S(2)}, u32[]{:S(2)}) collective-permute-start(bf16[64,8,2,128]{3,0,2,1:T(8,128)(2,1)S(1)} %get-tuple-element.38), channel_id=1, source_target_pairs={{0,4},{4,8},{8,12},{1,5},{5,9},{9,13},{2,6},{6,10},{10,14},{3,7},{... | collective-permute-start | bytes 786440 | tf_op jit(solution)/shard_map/ppermute | solution.py:12
  41.9 8.5 %collective-permute-start.5 = (bf16[64,8,2,128]{3,0,2,1:T(8,128)(2,1)S(1)}, bf16[64,8,2,128]{3,0,2,1:T(8,128)(2,1)S(1)}, u32[]{:S(2)}, u32[]{:S(2)}) collective-permute-start(bf16[64,8,2,128]{3,0,2,1:T(8,128)(2,1)S(1)} %get-tuple-element.39), channel_id=1, source_target_pairs={{4,0},{8,4},{12,8},{5,1},{9,5},{13,9},{6,2},{10,6},{14,10},{7,3},{... | collective-permute-start | bytes 786440 | tf_op jit(solution)/shard_map/ppermute | solution.py:15
  50.5 5.7 %collective-permute-start.6 = (bf16[64,2,12,128]{3,0,2,1:T(8,128)(2,1)S(1)}, bf16[64,2,12,128]{3,0,2,1:T(8,128)(2,1)S(1)}, u32[]{:S(2)}, u32[]{:S(2)}) collective-permute-start(bf16[64,2,12,128]{3,0,2,1:T(8,128)(2,1)S(1)} %get-tuple-element.34), channel_id=1, source_target_pairs={{0,1},{1,2},{2,3},{4,5},{5,6},{6,7},{8,9},{9,10},{10,11},{12,13},{... | collective-permute-start | bytes 1179656 | tf_op jit(solution)/shard_map/ppermute | solution.py:12
  54.8 4.1 %collective-permute-start.7 = (bf16[64,2,12,128]{3,0,2,1:T(8,128)(2,1)S(1)}, bf16[64,2,12,128]{3,0,2,1:T(8,128)(2,1)S(1)}, u32[]{:S(2)}, u32[]{:S(2)}) collective-permute-start(bf16[64,2,12,128]{3,0,2,1:T(8,128)(2,1)S(1)} %get-tuple-element.35), channel_id=1, source_target_pairs={{1,0},{2,1},{3,2},{5,4},{6,5},{7,6},{9,8},{10,9},{11,10},{13,12},{... | collective-permute-start | bytes 1179656 | tf_op jit(solution)/shard_map/ppermute | solution.py:15
  72.5 5.5 %copy-start.4 = (bf16[27,64,64]{2,1,0:T(8,128)(2,1)S(1)}, bf16[27,64,64]{2,1,0:T(8,128)(2,1)}, u32[]{:S(2)}) copy-start(bf16[27,64,64]{2,1,0:T(8,128)(2,1)} %param.9) | copy-start | bytes 663556
  81.9 8.2 %copy-start.2 = (f32[64]{0:T(128)S(1)}, f32[64]{0:T(128)}, u32[]{:S(2)}) copy-start(f32[64]{0:T(128)} %param.10) | copy-start | bytes 772
  92.4 14.4 %all-to-all-start = ((f32[1,64,8,128]{3,2,0,1:T(8,128)}), f32[1,64,8,128]{3,2,0,1:T(8,128)S(1)}, u32[]{:S(2)}, u32[]{:S(2)}) async-start(f32[1,64,8,128]{3,2,0,1:T(8,128)} %bitcast.340), calls=%async_computation | async-start | bytes 524288 | tf_op jit(solution)/shard_map/all_to_all | solution.py:69
where the time goes:
time: 108 us; the launch traced here: 107 us
  local copies, waits for them, and re-layouts  29.2 us (27%)
  starting transfers between devices  26.6 us (25%)
  waiting for transfers between devices  17.3 us (16%)
  matrix products  15.8 us (15%)
  other arithmetic  11 us (10%)
  blocking collectives  7.02 us (6%)
    unnamed x37, local copies, waits for them, and re-layouts  22.5 us
    dot_general x6, matrix products, convolve(): jnp.einsum('oc,czxy->ozxy', taps_flat, stacked, preferred_element_type=jn...  15.6 us
    ppermute x4, starting transfers between devices, extended(): lax.ppermute(lax.slice_in_dim(block, block.shape[dim] - width, None, axis...  14.1 us
    ppermute x4, waiting for transfers between devices, extended(): lax.ppermute(lax.slice_in_dim(block, 0, width, axis=dim), axis, backward)  13.3 us
    concatenate x3, other arithmetic, extended(): block = jnp.concatenate([low, block, high], axis=dim)  7.33 us
    all_to_all x1, starting transfers between devices, body(): lax.all_to_all(slab_image[None], 'depth', split_axis=1, concat_axis=0, ti...  7.27 us
    all_gather x1, blocking collectives, body(): depths_all = lax.all_gather(slab_depth[None], 'depth', axis=0, tiled=True)  7.02 us
    another operation x5, local copies, waits for them, and re-layouts, convolve(): jnp.stack(pieces, axis=0)  5.72 us
  transfers between devices with their start and end apart: 9, of which 6 were waited for; matrix products, arithmetic and copies ran while one was open for 2% of the time, Pallas kernels for 0%

commit v1 on v0

v1 whole, which is shorter than its diff:
```python
import functools

import jax
import jax.numpy as jnp
from jax import lax
from jax.experimental import pallas as pl
from jax.experimental.pallas import tpu as pltpu
from jax.sharding import PartitionSpec as P

BF16 = jnp.bfloat16
F32 = jnp.float32
HALO = 3
VMEM = pl.BlockSpec(memory_space=pltpu.VMEM)


def near_pairs(count):
    return [(i, i ^ 1) for i in range(count) if i ^ 1 < count]


def far_pairs(count):
    lows = [i for i in range(1, count - 1, 2)]
    return [(i, i + 1) for i in lows] + [(i + 1, i) for i in lows]


def swap_edges(block, axis, dim, width):
    index, count = lax.axis_index(axis), lax.axis_size(axis)
    last = block.shape[dim] - width
    even = index % 2 == 0
    near = lax.dynamic_slice_in_dim(block, jnp.where(even, last, 0), width, dim)
    far = lax.dynamic_slice_in_dim(block, jnp.where(even, 0, last), width, dim)
    return (
        lax.ppermute(near, axis, near_pairs(count)),
        lax.ppermute(far, axis, far_pairs(count)),
    )


def shifted_sum(parts, spacing, chans):
    lanes = parts.shape[1]
    column = lax.broadcasted_iota(jnp.int32, (chans, lanes), 1)
    low = pltpu.roll(parts[:chans], spacing, 1)
    high = pltpu.roll(parts[2 * chans :], lanes - spacing, 1)
    return (
        parts[chans : 2 * chans]
        + jnp.where(column >= spacing, low, 0.0)
        + jnp.where(column < lanes - spacing, high, 0.0)
    )


def silu(value):
    half = 0.5 * value
    return half + half * jnp.tanh(half)


def column_of(row_ref, lanes):
    chans = row_ref.shape[1]
    return jnp.broadcast_to(row_ref[...].astype(F32), (lanes, chans)).T


def pack_taps(source_ref, packed_ref):
    chans_out, chans_in = source_ref.shape[1:]
    for tap in range(9):
        packed_ref[:, tap * chans_in : (tap + 1) * chans_in] = source_ref[3 * tap : 3 * tap + 3].reshape(
            3 * chans_out, chans_in
        )


def conv_spots(taps_ref, fetch, spots, spacing, chans, lanes):
    blocks = []
    for dz in range(3):
        for dx in range(3):
            blocks.append(
                jnp.concatenate([fetch(z + spacing * dz, x + spacing * dx) for z, x in spots], axis=1)
            )
    stacked = jnp.concatenate(blocks, axis=0)
    parts = jnp.dot(taps_ref[...], stacked, preferred_element_type=F32)
    return [shifted_sum(parts[:, r * lanes : (r + 1) * lanes], spacing, chans) for r in range(len(spots))]


def edge_list(length):
    return [0, 1, 2, length + 1, length + 2, length + 3]


def inner_kernel(own_ref, w1_ref, b1_ref, w2_ref, hidden_ref, taps1_ref, taps2_ref):
    planes, rows, chans, lanes = own_ref.shape
    pack_taps(w1_ref, taps1_ref)
    bias = column_of(b1_ref, lanes)

    def step(plane, carry):
        for x in range(HALO, rows + 1, 2):
            spots = [(plane, x), (plane, x + 1)]
            sums = conv_spots(taps1_ref, lambda z, x: own_ref[z - HALO, x - HALO], spots, 1, chans, lanes)
            for (z, x), value in zip(spots, sums):
                hidden_ref[z, x] = silu(value + bias).astype(BF16)
        return carry

    lax.fori_loop(HALO, planes + 1, step, 0)
    pack_taps(w2_ref, taps2_ref)


def side_kernel(own_ref, tiles_ref, depths_ref, taps_ref, b1_ref, given_ref, hidden_ref):
    planes, rows, chans, lanes = own_ref.shape
    tile_odd, depth_odd = lax.axis_index("tile") % 2, lax.axis_index("depth") % 2
    bias = column_of(b1_ref, lanes)

    def fetch_x(z, x):
        if x < HALO:
            return tiles_ref[1 - tile_odd, z - HALO, x]
        if x >= rows + HALO:
            return tiles_ref[tile_odd, z - HALO, x - HALO - rows]
        return own_ref[z - HALO, x - HALO]

    def fetch_z(z, x):
        if z < HALO:
            return depths_ref[1 - depth_odd, z, x - HALO]
        if z >= planes + HALO:
            return depths_ref[depth_odd, z - HALO - planes, x - HALO]
        return own_ref[z - HALO, x - HALO]

    def emit(spots, fetch):
        sums = conv_spots(taps_ref, fetch, spots, 1, chans, lanes)
        for (z, x), value in zip(spots, sums):
            hidden_ref[z, x] = silu(value + bias).astype(BF16)

    edge_x, edge_z = edge_list(rows), edge_list(planes)

    def step_x(plane, carry):
        for i in range(0, len(edge_x), 2):
            emit([(plane, edge_x[i]), (plane, edge_x[i + 1])], fetch_x)
        return carry

    def step_z(pair, carry):
        x = HALO + 2 * pair
        for z in edge_z:
            emit([(z, x), (z, x + 1)], fetch_z)
        return carry

    lax.fori_loop(0, (rows - 2) // 2, step_z, 0)
    lax.fori_loop(HALO, planes + 1, step_x, 0)


def split_groups(value, bit, unit):
    groups = [value[i : i + unit] for i in range(0, value.shape[0], unit)]
    even, odd = jnp.concatenate(groups[0::2], axis=0), jnp.concatenate(groups[1::2], axis=0)
    return jnp.where(bit == 1, even, odd), jnp.where(bit == 1, odd, even)


def put_image(row, rows, image, depth, bit, unit, send_ref, keep_ref):
    send, keep = split_groups(image, bit, unit)
    width = send_ref.shape[1]
    for ref, value in ((send_ref, send), (keep_ref, keep)):
        ref[row] = value
        ref[rows + row // width, pl.ds(row % width, 1)] = depth


def field_kernel(
    tau_scale,
    unit,
    own_ref,
    tiles_ref,
    depths_ref,
    corners_ref,
    taps1_ref,
    b1_ref,
    taps2_ref,
    b2_ref,
    dens_ref,
    given_ref,
    hidden_ref,
    send_ref,
    keep_ref,
):
    planes, rows, chans, lanes = own_ref.shape
    tile_index, depth_index = lax.axis_index("tile"), lax.axis_index("depth")
    tile_odd, depth_odd = tile_index % 2, depth_index % 2
    bias1 = column_of(b1_ref, lanes)

    def fetch(z, x):
        side_z = 1 - depth_odd if z < HALO else depth_odd
        side_x = 1 - tile_odd if x < HALO else tile_odd
        in_z, in_x = z - HALO, x - HALO
        far_z, far_x = z if z < HALO else in_z - planes, x if x < HALO else in_x - rows
        if 0 <= in_z < planes:
            if 0 <= in_x < rows:
                return own_ref[in_z, in_x]
            return tiles_ref[side_x, in_z, far_x]
        if 0 <= in_x < rows:
            return depths_ref[side_z, far_z, in_x]
        return corners_ref[side_z, side_x, far_z, far_x]

    edge_x, edge_z = edge_list(rows), edge_list(planes)
    for z in edge_z:
        for i in range(0, len(edge_x), 2):
            spots = [(z, edge_x[i]), (z, edge_x[i + 1])]
            sums = conv_spots(taps1_ref, fetch, spots, 1, chans, lanes)
            for (_, x), value in zip(spots, sums):
                hidden_ref[z, x] = silu(value + bias1).astype(BF16)

    @pl.when(tile_index == 0)
    def _():
        hidden_ref[:, 0:2] = jnp.zeros((planes + 4, 2, chans, lanes), BF16)

    @pl.when(tile_index == lax.axis_size("tile") - 1)
    def _():
        hidden_ref[:, rows + 2 :] = jnp.zeros((planes + 4, 2, chans, lanes), BF16)

    @pl.when(depth_index == 0)
    def _():
        hidden_ref[0:2] = jnp.zeros((2, rows + 4, chans, lanes), BF16)

    @pl.when(depth_index == lax.axis_size("depth") - 1)
    def _():
        hidden_ref[planes + 2 :] = jnp.zeros((2, rows + 4, chans, lanes), BF16)

    bias2 = column_of(b2_ref, lanes)
    dens = column_of(dens_ref, lanes)

    def second(pair, carry):
        row = 2 * pair
        image = [jnp.zeros((chans, lanes), F32) for _ in range(2)]
        depth = [jnp.zeros((1, lanes), F32) for _ in range(2)]
        for plane in range(planes):
            sums = conv_spots(
                taps2_ref, lambda z, x: hidden_ref[z, x], [(plane, row), (plane, row + 1)], 2, chans, lanes
            )
            for r in range(2):
                feat = silu(sums[r] + bias2).astype(BF16).astype(F32)
                logit = jnp.sum(feat * dens, axis=0, keepdims=True)
                tau = jax.nn.softplus(logit) * tau_scale
                half = jnp.tanh(0.5 * tau)
                weight = (jnp.exp(-depth[r]) * (2.0 * half / (1.0 + half))).astype(BF16).astype(F32)
                image[r] = image[r] + weight * feat
                depth[r] = depth[r] + tau
        for r in range(2):
            put_image(row + r, rows, image[r], depth[r], depth_odd, unit, send_ref, keep_ref)
        return carry

    lax.fori_loop(0, rows // 2, second, 0)


def merge_rows(rows, mine_ref, other_ref, bit):
    width = mine_ref.shape[1]
    front = bit == 0
    for row in range(rows):
        spot = (rows + row // width, slice(row % width, row % width + 1))
        mine_depth, other_depth = mine_ref[spot], other_ref[spot]
        mine_scale = jnp.where(front, 1.0, jnp.exp(-other_depth))
        other_scale = jnp.where(front, jnp.exp(-mine_depth), 1.0)
        yield row, mine_scale * mine_ref[row] + other_scale * other_ref[row], mine_depth + other_depth


def merge_kernel(rows, level, unit, mine_ref, other_ref, send_ref, keep_ref):
    index = lax.axis_index("depth")
    bit, later = lax.rem(lax.div(index, 1 << level), 2), lax.rem(lax.div(index, 2 << level), 2)
    for row, image, depth in merge_rows(rows, mine_ref, other_ref, bit):
        put_image(row, rows, image, depth, later, unit, send_ref, keep_ref)


def last_kernel(rows, level, mine_ref, other_ref, out_ref):
    bit = lax.rem(lax.div(lax.axis_index("depth"), 1 << level), 2)
    for row, image, _ in merge_rows(rows, mine_ref, other_ref, bit):
        out_ref[:, row] = image


def call(kernel, name, outs, args, flops, limit, aliases=None, scratch=()):
    return pl.pallas_call(
        kernel,
        out_shape=outs,
        in_specs=[VMEM] * len(args),
        out_specs=jax.tree.map(lambda _: VMEM, outs),
        scratch_shapes=scratch,
        input_output_aliases=aliases or {},
        compiler_params=pltpu.CompilerParams(vmem_limit_bytes=limit << 20),
        cost_estimate=pl.CostEstimate(flops=flops, bytes_accessed=1 << 20, transcendentals=0),
        name=name,
    )(*args)


def body(volume, first_kernel, first_bias, second_kernel, second_bias, density_weight):
    chans, planes, rows, lanes = volume.shape
    count = lax.axis_size("depth")
    unit = chans // count
    levels = count.bit_length() - 1
    assert count == 1 << levels and count > 1
    own = volume.transpose(1, 2, 0, 3)
    tiles = jnp.stack(swap_edges(own, "tile", 1, HALO))
    depths = jnp.stack(swap_edges(own, "depth", 0, HALO))
    corners = jnp.stack(swap_edges(tiles, "depth", 1, HALO))
    b1, b2, dens = first_bias[None], second_bias[None], density_weight[None]

    row_flops = 2 * 27 * chans * chans * lanes
    hidden_shape = jax.ShapeDtypeStruct((planes + 4, rows + 4, chans, lanes), BF16)
    taps_shape = jax.ShapeDtypeStruct((3 * chans, 9 * chans), BF16)
    inner, sides = (planes - 2) * (rows - 2), 6 * (planes + rows - 4)
    hidden, taps1, taps2 = call(
        inner_kernel,
        "inner",
        (hidden_shape, taps_shape, taps_shape),
        (own, first_kernel, b1, second_kernel),
        row_flops * inner,
        12,
    )
    hidden = call(
        side_kernel, "sides", hidden_shape, (own, tiles, depths, taps1, b1, hidden), row_flops * sides, 12, {5: 0}
    )

    def image_shape(width):
        return jax.ShapeDtypeStruct((rows + -(-rows // width), width, lanes), F32)

    half = image_shape(chans // 2)
    _, send, keep = call(
        functools.partial(field_kernel, 2.0 / (planes * count), unit),
        "field",
        (hidden_shape, half, half),
        (own, tiles, depths, corners, taps1, b1, taps2, b2, dens, hidden),
        row_flops * (36 + planes * rows),
        12,
        {9: 0},
    )
    for level in range(levels):
        got = lax.ppermute(send, "depth", [(i, i ^ (1 << level)) for i in range(count)])
        if level < levels - 1:
            part = image_shape(send.shape[1] // 2)
            send, keep = call(
                functools.partial(merge_kernel, rows, level, unit), "merge", (part, part), (keep, got), 1 << 20, 4
            )
    return call(
        functools.partial(last_kernel, rows, levels - 1),
        "last",
        jax.ShapeDtypeStruct((unit, rows, lanes), F32),
        (keep, got),
        1 << 20,
        4,
    )


def solution(mesh):
    placed = (P(None, ("groups", "depth"), "tile", None), P(), P(), P(), P(), P())
    return jax.shard_map(
        body,
        mesh=mesh,
        in_specs=placed,
        out_specs=P("depth", ("groups", "tile"), None),
        check_vma=False,
    )
```

time: 108 us -> 37.7 us (0.35)
  the two profiles are of different devices: /device:TPU:0 before, /device:TPU:20 now
where the time goes in v1:
time: 37.7 us; the launch traced here: 37.5 us
  Pallas kernels  15 us (40%)
  waiting for transfers between devices  11 us (29%)
  starting transfers between devices  8.88 us (24%)
  local copies, waits for them, and re-layouts  2.15 us (6%)
    pallas_call x5, Pallas kernels, call(): pl.pallas_call(kernel, out_shape=outs, in_specs=[VMEM] * len(args), out_s...  15 us
    ppermute x2, waiting for transfers between devices, body(): lax.ppermute(send, 'depth', [(i, i ^ 1 << level) for i in range(count)])  4.65 us
    ppermute x2, starting transfers between devices, body(): lax.ppermute(send, 'depth', [(i, i ^ 1 << level) for i in range(count)])  3.82 us
    ppermute x3, starting transfers between devices, swap_edges(): lax.ppermute(far, axis, far_pairs(count))  3.27 us
    ppermute x3, waiting for transfers between devices, swap_edges(): lax.ppermute(far, axis, far_pairs(count))  3.18 us
    ppermute x3, waiting for transfers between devices, swap_edges(): lax.ppermute(near, axis, near_pairs(count))  3.18 us
    unnamed x11, local copies, waits for them, and re-layouts  2.01 us
    ppermute x3, starting transfers between devices, swap_edges(): lax.ppermute(near, axis, near_pairs(count))  1.78 us
  transfers between devices with their start and end apart: 8, of which 4 were waited for; matrix products, arithmetic and copies ran while one was open for 1% of the time, Pallas kernels for 23%

profile of v1, /device:TPU:20, one launch (start us, length us, event | category | flops | bytes accessed | tf_op | source)
XLA Modules:
  0.0 37.5 jit_solution(3456252566016904226)
XLA Ops:
  0.0 2.0 %copy.16 = bf16[64,8,8,128]{3,0,2,1:T(8,128)(2,1)S(1)} copy(bf16[64,8,8,128]{3,2,1,0:T(8,128)(2,1)} %param.6) | data formatting | bytes 2097152 | tf_op args[0]
  2.0 0.1 dynamic-slice_bitcast_fusion.3
  2.1 1.6 %collective-permute-start = (bf16[8,3,64,128]{3,2,1,0:T(8,128)(2,1)S(1)}, bf16[8,3,64,128]{3,2,1,0:T(8,128)(2,1)S(1)}, u32[]{:S(2)}, u32[]{:S(2)}) collective-permute-start(bf16[8,3,64,128]{3,2,1,0:T(8,128)(2,1)S(1)} %get-tuple-element.21), channel_id=1, source_target_pairs={{0,4},{4,0},{8,12},{12,8},{1,5},{5,1},{9,13},{13,9},{2,6},{6,2},{1... | collective-permute-start | bytes 1179656 | tf_op jit(solution)/shard_map/ppermute | solution.py:32
  3.7 1.9 %collective-permute-start.1 = (bf16[8,3,64,128]{3,2,1,0:T(8,128)(2,1)S(1)}, bf16[8,3,64,128]{3,2,1,0:T(8,128)(2,1)S(1)}, u32[]{:S(2)}, u32[]{:S(2)}) collective-permute-start(bf16[8,3,64,128]{3,2,1,0:T(8,128)(2,1)S(1)} %get-tuple-element.22), channel_id=1, source_target_pairs={{4,8},{8,4},{5,9},{9,5},{6,10},{10,6},{7,11},{11,7},{20,24},{24,20... | collective-permute-start | bytes 1179656 | tf_op jit(solution)/shard_map/ppermute | solution.py:33
  5.6 0.1 dynamic-slice_bitcast_fusion.1
  5.7 0.1 collective-permute-start.2
  5.8 0.7 %collective-permute-start.3 = (bf16[3,8,64,128]{3,2,1,0:T(8,128)(2,1)S(1)}, bf16[3,8,64,128]{3,2,1,0:T(8,128)(2,1)S(1)}, u32[]{:S(2)}, u32[]{:S(2)}) collective-permute-start(bf16[3,8,64,128]{3,2,1,0:T(8,128)(2,1)S(1)} %get-tuple-element.20), channel_id=1, source_target_pairs={{1,2},{2,1},{5,6},{6,5},{9,10},{10,9},{13,14},{14,13},{17,18},{18,... | collective-permute-start | bytes 1179656 | tf_op jit(solution)/shard_map/ppermute | solution.py:33
  6.5 0.0 copy-done
  6.5 0.0 copy-done.1
  6.5 0.0 copy-done.2
  6.5 3.3 %inner.1 = (bf16[12,12,64,128]{3,2,1,0:T(8,128)(2,1)S(1)}, bf16[192,576]{1,0:T(8,128)(2,1)S(1)}, bf16[192,576]{1,0:T(8,128)(2,1)S(1)}) custom-call(bf16[8,8,64,128]{3,2,1,0:T(8,128)(2,1)S(1)} %bitcast.19, bf16[27,64,64]{2,1,0:T(8,128)(2,1)S(1)} %copy-done.1, f32[1,64]{1,0:T(1,128)S(1)} %bitcast.22, bf16[27,64,64]{2,1,0:T(8,128)(2,1)S(1)} %copy-done.2), custom_call_target="tpu_custom_call" | custom-call | flops 1019215872 | bytes 1048576 | tf_op jit(solution)/shard_map/inner/pallas_call | solution.py:265
  9.8 3.2 %collective-permute-done = bf16[8,3,64,128]{3,2,1,0:T(8,128)(2,1)S(1)} collective-permute-done((bf16[8,3,64,128]{3,2,1,0:T(8,128)(2,1)S(1)}, bf16[8,3,64,128]{3,2,1,0:T(8,128)(2,1)S(1)}, u32[]{:S(2)}, u32[]{:S(2)}) %collective-permute-start) | collective-permute-done | bytes 393248 | tf_op jit(solution)/shard_map/ppermute | solution.py:32
  13.0 3.2 %collective-permute-done.1 = bf16[8,3,64,128]{3,2,1,0:T(8,128)(2,1)S(1)} collective-permute-done((bf16[8,3,64,128]{3,2,1,0:T(8,128)(2,1)S(1)}, bf16[8,3,64,128]{3,2,1,0:T(8,128)(2,1)S(1)}, u32[]{:S(2)}, u32[]{:S(2)}) %collective-permute-start.1) | collective-permute-done | bytes 393248 | tf_op jit(solution)/shard_map/ppermute | solution.py:33
  16.2 0.1 fusion
  16.2 0.1 collective-permute-start.4
  16.3 0.7 %collective-permute-start.5 = (bf16[2,3,3,64,128]{4,3,2,1,0:T(8,128)(2,1)S(1)}, bf16[2,3,3,64,128]{4,3,2,1,0:T(8,128)(2,1)S(1)}, u32[]{:S(2)}, u32[]{:S(2)}) collective-permute-start(bf16[2,3,3,64,128]{4,3,2,1,0:T(8,128)(2,1)S(1)} %get-tuple-element.26), channel_id=1, source_target_pairs={{1,2},{2,1},{5,6},{6,5},{9,10},{10,9},{13,14},{14,13},{17,18},{18,... | collective-permute-start | bytes 884744 | tf_op jit(solution)/shard_map/ppermute | solution.py:33
  17.0 0.1 pad_maximum_fusion.tiles_ref
  17.1 0.0 collective-permute-done.2
  17.1 0.0 collective-permute-done.3
  17.1 0.1 pad_maximum_fusion.1.depths_ref
  17.2 0.0 copy-start.3
  17.2 0.0 copy-start.4
  17.2 5.2 %sides.1.given_ref = bf16[12,12,64,128]{3,2,1,0:T(8,128)(2,1)S(1)} custom-call(bf16[8,8,64,128]{3,2,1,0:T(8,128)(2,1)S(1)} %bitcast.20, bf16[2,8,3,64,128]{4,3,2,1,0:T(8,128)(2,1)S(1)} %pad_maximum_fusion.tiles_ref, bf16[2,3,8,64,128]{4,3,2,1,0:T(8,128)(2,1)S(1)} %pad_maximum_fusion.1.depths_ref, ...), custom_call_target="tpu_custom_call", output_to_operand_aliasing={{}: (5, {})} | custom-call | flops 2038431744 | bytes 1048576 | tf_op jit(solution)/shard_map/sides/pallas_call | solution.py:265
  22.4 0.0 collective-permute-done.4
  22.5 0.0 collective-permute-done.5
  22.5 0.1 pad_maximum_fusion.2.corners_ref
  22.6 5.7 %field.1 = (bf16[12,12,64,128]{3,2,1,0:T(8,128)(2,1)S(1)}, f32[9,32,128]{2,1,0:T(8,128)S(1)}, f32[9,32,128]{2,1,0:T(8,128)S(1)}) custom-call(bf16[8,8,64,128]{3,2,1,0:T(8,128)(2,1)S(1)} %bitcast.21, bf16[2,8,3,64,128]{4,3,2,1,0:T(8,128)(2,1)S(1)} %pad_maximum_fusion.tiles_ref, ...), custom_call_target="tpu_custom_call", output_to_operand_aliasing={{0}: (9, {})} | custom-call | flops 2831155200 | bytes 1048576 | tf_op jit(solution)/shard_map/field/pallas_call | solution.py:265
  28.3 2.9 %collective-permute-start.6 = (f32[9,32,128]{2,1,0:T(8,128)S(1)}, f32[9,32,128]{2,1,0:T(8,128)S(1)}, u32[]{:S(2)}, u32[]{:S(2)}) collective-permute-start(f32[9,32,128]{2,1,0:T(8,128)S(1)} %get-tuple-element.16), channel_id=1, source_target_pairs={{0,1},{1,0},{2,3},{3,2},{4,5},{5,4},{6,7},{7,6},{8,9},{9,8},{10,11... | collective-permute-start | bytes 442376 | tf_op jit(solution)/shard_map/ppermute | solution.py:320
  31.1 1.0 %collective-permute-done.6.other_ref = f32[9,32,128]{2,1,0:T(8,128)S(1)} collective-permute-done((f32[9,32,128]{2,1,0:T(8,128)S(1)}, f32[9,32,128]{2,1,0:T(8,128)S(1)}, u32[]{:S(2)}, u32[]{:S(2)}) %collective-permute-start.6) | collective-permute-done | bytes 147488 | tf_op jit(solution)/shard_map/ppermute | solution.py:320
  32.2 1.0 %collective-permute-start.7 = (f32[9,16,128]{2,1,0:T(8,128)S(1)}, f32[9,16,128]{2,1,0:T(8,128)S(1)}, u32[]{:S(2)}, u32[]{:S(2)}) collective-permute-start(f32[9,16,128]{2,1,0:T(8,128)S(1)} %get-tuple-element.18), channel_id=1, source_target_pairs={{0,2},{1,3},{2,0},{3,1},{4,6},{5,7},{6,4},{7,5},{8,10},{9,11},{10,... | collective-permute-start | bytes 221192 | tf_op jit(solution)/shard_map/ppermute | solution.py:320
  33.2 3.6 %collective-permute-done.7.other_ref = f32[9,16,128]{2,1,0:T(8,128)S(1)} collective-permute-done((f32[9,16,128]{2,1,0:T(8,128)S(1)}, f32[9,16,128]{2,1,0:T(8,128)S(1)}, u32[]{:S(2)}, u32[]{:S(2)}) %collective-permute-start.7) | collective-permute-done | bytes 73760 | tf_op jit(solution)/shard_map/ppermute | solution.py:320
  36.8 0.7 %last.1 = f32[16,8,128]{2,1,0:T(8,128)} custom-call(f32[9,16,128]{2,1,0:T(8,128)S(1)} %get-tuple-element.17.mine_ref, f32[9,16,128]{2,1,0:T(8,128)S(1)} %collective-permute-done.7.other_ref), custom_call_target="tpu_custom_call" | custom-call | flops 1048576 | bytes 1048576 | tf_op jit(solution)/shard_map/last/pallas_call | solution.py:265
  (6 shorter events, 0.1 us)
Async XLA Ops:
  0.0 6.5 %copy-start = (f32[64]{0:T(128)S(1)}, f32[64]{0:T(128)}, u32[]{:S(2)}) copy-start(f32[64]{0:T(128)} %param.8) | copy-start | bytes 772
  0.0 6.5 %copy-start.1 = (bf16[27,64,64]{2,1,0:T(8,128)(2,1)S(1)}, bf16[27,64,64]{2,1,0:T(8,128)(2,1)}, u32[]{:S(2)}) copy-start(bf16[27,64,64]{2,1,0:T(8,128)(2,1)} %w1_ref.1) | copy-start | bytes 663556
  0.0 6.5 %copy-start.2 = (bf16[27,64,64]{2,1,0:T(8,128)(2,1)S(1)}, bf16[27,64,64]{2,1,0:T(8,128)(2,1)}, u32[]{:S(2)}) copy-start(bf16[27,64,64]{2,1,0:T(8,128)(2,1)} %w2_ref.1) | copy-start | bytes 663556
  2.1 10.9 %collective-permute-start = (bf16[8,3,64,128]{3,2,1,0:T(8,128)(2,1)S(1)}, bf16[8,3,64,128]{3,2,1,0:T(8,128)(2,1)S(1)}, u32[]{:S(2)}, u32[]{:S(2)}) collective-permute-start(bf16[8,3,64,128]{3,2,1,0:T(8,128)(2,1)S(1)} %get-tuple-element.21), channel_id=1, source_target_pairs={{0,4},{4,0},{8,12},{12,8},{1,5},{5,1},{9,13},{13,9},{2,6},{6,2},{1... | collective-permute-start | bytes 1179656 | tf_op jit(solution)/shard_map/ppermute | solution.py:32
  3.7 12.5 %collective-permute-start.1 = (bf16[8,3,64,128]{3,2,1,0:T(8,128)(2,1)S(1)}, bf16[8,3,64,128]{3,2,1,0:T(8,128)(2,1)S(1)}, u32[]{:S(2)}, u32[]{:S(2)}) collective-permute-start(bf16[8,3,64,128]{3,2,1,0:T(8,128)(2,1)S(1)} %get-tuple-element.22), channel_id=1, source_target_pairs={{4,8},{8,4},{5,9},{9,5},{6,10},{10,6},{7,11},{11,7},{20,24},{24,20... | collective-permute-start | bytes 1179656 | tf_op jit(solution)/shard_map/ppermute | solution.py:33
  5.7 11.3 %collective-permute-start.2 = (bf16[3,8,64,128]{3,2,1,0:T(8,128)(2,1)S(1)}, bf16[3,8,64,128]{3,2,1,0:T(8,128)(2,1)S(1)}, u32[]{:S(2)}, u32[]{:S(2)}) collective-permute-start(bf16[3,8,64,128]{3,2,1,0:T(8,128)(2,1)S(1)} %get-tuple-element.19), channel_id=1, source_target_pairs={{0,1},{1,0},{2,3},{3,2},{4,5},{5,4},{6,7},{7,6},{8,9},{9,8},{10,11... | collective-permute-start | bytes 1179656 | tf_op jit(solution)/shard_map/ppermute | solution.py:32
  5.8 11.3 %collective-permute-start.3 = (bf16[3,8,64,128]{3,2,1,0:T(8,128)(2,1)S(1)}, bf16[3,8,64,128]{3,2,1,0:T(8,128)(2,1)S(1)}, u32[]{:S(2)}, u32[]{:S(2)}) collective-permute-start(bf16[3,8,64,128]{3,2,1,0:T(8,128)(2,1)S(1)} %get-tuple-element.20), channel_id=1, source_target_pairs={{1,2},{2,1},{5,6},{6,5},{9,10},{10,9},{13,14},{14,13},{17,18},{18,... | collective-permute-start | bytes 1179656 | tf_op jit(solution)/shard_map/ppermute | solution.py:33
  16.2 6.2 %collective-permute-start.4 = (bf16[2,3,3,64,128]{4,3,2,1,0:T(8,128)(2,1)S(1)}, bf16[2,3,3,64,128]{4,3,2,1,0:T(8,128)(2,1)S(1)}, u32[]{:S(2)}, u32[]{:S(2)}) collective-permute-start(bf16[2,3,3,64,128]{4,3,2,1,0:T(8,128)(2,1)S(1)} %get-tuple-element.25), channel_id=1, source_target_pairs={{0,1},{1,0},{2,3},{3,2},{4,5},{5,4},{6,7},{7,6},{8,9},{9,8},{10,11... | collective-permute-start | bytes 884744 | tf_op jit(solution)/shard_map/ppermute | solution.py:32
  16.3 6.2 %collective-permute-start.5 = (bf16[2,3,3,64,128]{4,3,2,1,0:T(8,128)(2,1)S(1)}, bf16[2,3,3,64,128]{4,3,2,1,0:T(8,128)(2,1)S(1)}, u32[]{:S(2)}, u32[]{:S(2)}) collective-permute-start(bf16[2,3,3,64,128]{4,3,2,1,0:T(8,128)(2,1)S(1)} %get-tuple-element.26), channel_id=1, source_target_pairs={{1,2},{2,1},{5,6},{6,5},{9,10},{10,9},{13,14},{14,13},{17,18},{18,... | collective-permute-start | bytes 884744 | tf_op jit(solution)/shard_map/ppermute | solution.py:33
  17.2 5.4 %copy-start.3 = (f32[64]{0:T(128)S(1)}, f32[64]{0:T(128)}, u32[]{:S(2)}) copy-start(f32[64]{0:T(128)} %param.10) | copy-start | bytes 772
  17.2 5.4 %copy-start.4 = (bf16[64]{0:T(256)(128)(2,1)S(1)}, bf16[64]{0:T(256)(128)(2,1)}, u32[]{:S(2)}) copy-start(bf16[64]{0:T(256)(128)(2,1)} %param.11) | copy-start | bytes 388
  28.3 3.9 %collective-permute-start.6 = (f32[9,32,128]{2,1,0:T(8,128)S(1)}, f32[9,32,128]{2,1,0:T(8,128)S(1)}, u32[]{:S(2)}, u32[]{:S(2)}) collective-permute-start(f32[9,32,128]{2,1,0:T(8,128)S(1)} %get-tuple-element.16), channel_id=1, source_target_pairs={{0,1},{1,0},{2,3},{3,2},{4,5},{5,4},{6,7},{7,6},{8,9},{9,8},{10,11... | collective-permute-start | bytes 442376 | tf_op jit(solution)/shard_map/ppermute | solution.py:320
  32.2 4.6 %collective-permute-start.7 = (f32[9,16,128]{2,1,0:T(8,128)S(1)}, f32[9,16,128]{2,1,0:T(8,128)S(1)}, u32[]{:S(2)}, u32[]{:S(2)}) collective-permute-start(f32[9,16,128]{2,1,0:T(8,128)S(1)} %get-tuple-element.18), channel_id=1, source_target_pairs={{0,2},{1,3},{2,0},{3,1},{4,6},{5,7},{6,4},{7,5},{8,10},{9,11},{10,... | collective-permute-start | bytes 221192 | tf_op jit(solution)/shard_map/ppermute | solution.py:320

commit v2 on v1

--- a/solution.py
+++ b/solution.py
@@ -22,16 +22,64 @@
     return [(i, i + 1) for i in lows] + [(i + 1, i) for i in lows]
 
 
-def swap_edges(block, axis, dim, width):
-    index, count = lax.axis_index(axis), lax.axis_size(axis)
-    last = block.shape[dim] - width
-    even = index % 2 == 0
-    near = lax.dynamic_slice_in_dim(block, jnp.where(even, last, 0), width, dim)
-    far = lax.dynamic_slice_in_dim(block, jnp.where(even, 0, last), width, dim)
-    return (
-        lax.ppermute(near, axis, near_pairs(count)),
-        lax.ppermute(far, axis, far_pairs(count)),
-    )
+def partners(axis, far):
+    count = lax.axis_size(axis)
+    return far_pairs(count) if far else near_pairs(count)
+
+
+def swap(block, axis, far):
+    return lax.ppermute(block, axis, partners(axis, far))
+
+
+def swap_corner(block, far):
+    count = lax.axis_size("depth")
+    pairs = [
+        (a * count + b, c * count + d) for a, c in partners("tile", far) for b, d in partners("depth", True)
+    ]
+    return lax.ppermute(block, ("tile", "depth"), pairs)
+
+
+def spread_kernel(volume_ref, *refs):
+    given_refs, (own_ref, tn_ref, tf_ref, dn_ref, df_ref, cn_ref, cf_ref), kept_refs = (
+        refs[:5],
+        refs[5:12],
+        refs[12:17],
+    )
+    raw_ref, wide_ref, sems, kept_sems = refs[17:]
+    planes, rows, chans, lanes = own_ref.shape
+    copies = [
+        pltpu.make_async_copy(volume_ref.at[:, z], raw_ref.at[z], sems.at[z]) for z in range(planes)
+    ]
+    others = [
+        pltpu.make_async_copy(given, kept, kept_sems.at[i])
+        for i, (given, kept) in enumerate(zip(given_refs, kept_refs))
+    ]
+    for copy in copies + others:
+        copy.start()
+    for z in range(planes):
+        copies[z].wait()
+        wide_ref[z % 2] = raw_ref[z].astype(F32).reshape(chans * rows, lanes)
+        for x in range(rows):
+            own_ref[z, x] = wide_ref[z % 2, pl.ds(x, chans, stride=rows), :].astype(BF16)
+    tile_odd, depth_odd = lax.axis_index("tile") % 2, lax.axis_index("depth") % 2
+    near_x, far_x = (1 - tile_odd) * (rows - HALO), tile_odd * (rows - HALO)
+    near_z, far_z = (1 - depth_odd) * (planes - HALO), depth_odd * (planes - HALO)
+    tn_ref[...] = own_ref[:, pl.ds(near_x, HALO)]
+    tf_ref[...] = own_ref[:, pl.ds(far_x, HALO)]
+    dn_ref[...] = own_ref[pl.ds(near_z, HALO)]
+    df_ref[...] = own_ref[pl.ds(far_z, HALO)]
+    cn_ref[...] = own_ref[pl.ds(far_z, HALO), pl.ds(near_x, HALO)]
+    cf_ref[...] = own_ref[pl.ds(far_z, HALO), pl.ds(far_x, HALO)]
+    for copy in others:
+        copy.wait()
+
+
+def cut_kernel(near_ref, far_ref, both_ref, given_ref):
+    planes = near_ref.shape[0]
+    start = (1 - lax.axis_index("depth") % 2) * (planes - HALO)
+    for i, ref in enumerate((near_ref, far_ref)):
+        given_ref[i] = ref[pl.ds(start, HALO)]
+        both_ref[i] = ref[...]
 
 
 def shifted_sum(parts, spacing, chans):
@@ -85,57 +133,41 @@
     pack_taps(w1_ref, taps1_ref)
     bias = column_of(b1_ref, lanes)
 
-    def step(plane, carry):
+    for plane in range(HALO, planes + 1):
         for x in range(HALO, rows + 1, 2):
             spots = [(plane, x), (plane, x + 1)]
             sums = conv_spots(taps1_ref, lambda z, x: own_ref[z - HALO, x - HALO], spots, 1, chans, lanes)
             for (z, x), value in zip(spots, sums):
                 hidden_ref[z, x] = silu(value + bias).astype(BF16)
-        return carry
-
-    lax.fori_loop(HALO, planes + 1, step, 0)
     pack_taps(w2_ref, taps2_ref)
 
 
-def side_kernel(own_ref, tiles_ref, depths_ref, taps_ref, b1_ref, given_ref, hidden_ref):
+def side_spots(axis, planes, rows):
+    if axis == "tile":
+        edges = edge_list(rows)
+        return [
+            [(z, edges[i]), (z, edges[i + 1])] for z in range(HALO, planes + 1) for i in range(0, len(edges), 2)
+        ]
+    return [[(z, x), (z, x + 1)] for x in range(HALO, rows + 1, 2) for z in edge_list(planes)]
+
+
+def side_kernel(axis, own_ref, halo_ref, taps_ref, b1_ref, given_ref, hidden_ref):
     planes, rows, chans, lanes = own_ref.shape
-    tile_odd, depth_odd = lax.axis_index("tile") % 2, lax.axis_index("depth") % 2
+    odd = lax.axis_index(axis) % 2
     bias = column_of(b1_ref, lanes)
 
-    def fetch_x(z, x):
-        if x < HALO:
-            return tiles_ref[1 - tile_odd, z - HALO, x]
-        if x >= rows + HALO:
-            return tiles_ref[tile_odd, z - HALO, x - HALO - rows]
-        return own_ref[z - HALO, x - HALO]
-
-    def fetch_z(z, x):
-        if z < HALO:
-            return depths_ref[1 - depth_odd, z, x - HALO]
-        if z >= planes + HALO:
-            return depths_ref[depth_odd, z - HALO - planes, x - HALO]
-        return own_ref[z - HALO, x - HALO]
-
-    def emit(spots, fetch):
+    def fetch(z, x):
+        in_z, in_x = z - HALO, x - HALO
+        along, length = (in_x, rows) if axis == "tile" else (in_z, planes)
+        if 0 <= along < length:
+            return own_ref[in_z, in_x]
+        side, far = (1 - odd, along + HALO) if along < 0 else (odd, along - length)
+        return halo_ref[side, in_z, far] if axis == "tile" else halo_ref[side, far, in_x]
+
+    for spots in side_spots(axis, planes, rows):
         sums = conv_spots(taps_ref, fetch, spots, 1, chans, lanes)
         for (z, x), value in zip(spots, sums):
             hidden_ref[z, x] = silu(value + bias).astype(BF16)
-
-    edge_x, edge_z = edge_list(rows), edge_list(planes)
-
-    def step_x(plane, carry):
-        for i in range(0, len(edge_x), 2):
-            emit([(plane, edge_x[i]), (plane, edge_x[i + 1])], fetch_x)
-        return carry
-
-    def step_z(pair, carry):
-        x = HALO + 2 * pair
-        for z in edge_z:
-            emit([(z, x), (z, x + 1)], fetch_z)
-        return carry
-
-    lax.fori_loop(0, (rows - 2) // 2, step_z, 0)
-    lax.fori_loop(HALO, planes + 1, step_x, 0)
 
 
 def split_groups(value, bit, unit):
@@ -214,8 +246,7 @@
     bias2 = column_of(b2_ref, lanes)
     dens = column_of(dens_ref, lanes)
 
-    def second(pair, carry):
-        row = 2 * pair
+    for row in range(0, rows, 2):
         image = [jnp.zeros((chans, lanes), F32) for _ in range(2)]
         depth = [jnp.zeros((1, lanes), F32) for _ in range(2)]
         for plane in range(planes):
@@ -232,9 +263,6 @@
                 depth[r] = depth[r] + tau
         for r in range(2):
             put_image(row + r, rows, image[r], depth[r], depth_odd, unit, send_ref, keep_ref)
-        return carry
-
-    lax.fori_loop(0, rows // 2, second, 0)
 
 
 def merge_rows(rows, mine_ref, other_ref, bit):
@@ -261,17 +289,16 @@
         out_ref[:, row] = image
 
 
-def call(kernel, name, outs, args, flops, limit, aliases=None, scratch=()):
+def call(kernel, outs, args, flops, limit, aliases=None, scratch=(), space=pltpu.VMEM):
     return pl.pallas_call(
         kernel,
         out_shape=outs,
-        in_specs=[VMEM] * len(args),
+        in_specs=[pl.BlockSpec(memory_space=space)] * len(args),
         out_specs=jax.tree.map(lambda _: VMEM, outs),
         scratch_shapes=scratch,
         input_output_aliases=aliases or {},
         compiler_params=pltpu.CompilerParams(vmem_limit_bytes=limit << 20),
         cost_estimate=pl.CostEstimate(flops=flops, bytes_accessed=1 << 20, transcendentals=0),
-        name=name,
     )(*args)
 
 
@@ -281,27 +308,57 @@
     unit = chans // count
     levels = count.bit_length() - 1
     assert count == 1 << levels and count > 1
-    own = volume.transpose(1, 2, 0, 3)
-    tiles = jnp.stack(swap_edges(own, "tile", 1, HALO))
-    depths = jnp.stack(swap_edges(own, "depth", 0, HALO))
-    corners = jnp.stack(swap_edges(tiles, "depth", 1, HALO))
-    b1, b2, dens = first_bias[None], second_bias[None], density_weight[None]
+
+    def field_shape(*dims):
+        return jax.ShapeDtypeStruct(dims + (chans, lanes), BF16)
+
+    tile_edge, depth_edge, corner = field_shape(planes, HALO), field_shape(HALO, rows), field_shape(HALO, HALO)
+    params = (first_kernel, second_kernel, first_bias[None], second_bias[None], density_weight[None])
+    own, tn, tf, dn, df, cn, cf, w1, w2, b1, b2, dens = call(
+        spread_kernel,
+        (field_shape(planes, rows), tile_edge, tile_edge, depth_edge, depth_edge, corner, corner)
+        + tuple(jax.ShapeDtypeStruct(p.shape, p.dtype) for p in params),
+        tuple(pltpu.with_memory_space_constraint(p, pltpu.HBM) for p in (volume,) + params),
+        1 << 20,
+        12,
+        scratch=[
+            pltpu.VMEM((planes, chans, rows, lanes), BF16),
+            pltpu.VMEM((2, chans * rows, lanes), F32),
+            pltpu.SemaphoreType.DMA((planes,)),
+            pltpu.SemaphoreType.DMA((len(params),)),
+        ],
+        space=pltpu.HBM,
+    )
+    tiles, given = call(
+        cut_kernel,
+        (
+            jax.ShapeDtypeStruct((2, planes, HALO, chans, lanes), BF16),
+            jax.ShapeDtypeStruct((2, HALO, HALO, chans, lanes), BF16),
+        ),
+        (swap(tn, "tile", False), swap(tf, "tile", True)),
+        1 << 20,
+        4,
+    )
+    far_corners = jnp.stack([swap_corner(cn, False), swap_corner(cf, True)])
+    depths = jnp.stack([swap(dn, "depth", False), swap(df, "depth", True)])
+    corners = jnp.stack([swap(given, "depth", False), far_corners])
 
     row_flops = 2 * 27 * chans * chans * lanes
     hidden_shape = jax.ShapeDtypeStruct((planes + 4, rows + 4, chans, lanes), BF16)
     taps_shape = jax.ShapeDtypeStruct((3 * chans, 9 * chans), BF16)
-    inner, sides = (planes - 2) * (rows - 2), 6 * (planes + rows - 4)
+    inner = (planes - 2) * (rows - 2)
     hidden, taps1, taps2 = call(
-        inner_kernel,
-        "inner",
-        (hidden_shape, taps_shape, taps_shape),
-        (own, first_kernel, b1, second_kernel),
-        row_flops * inner,
-        12,
-    )
-    hidden = call(
-        side_kernel, "sides", hidden_shape, (own, tiles, depths, taps1, b1, hidden), row_flops * sides, 12, {5: 0}
-    )
+        inner_kernel, (hidden_shape, taps_shape, taps_shape), (own, w1, b1, w2), row_flops * inner, 12
+    )
+    for axis, halo, count_rows in (("depth", depths, 6 * (rows - 2)), ("tile", tiles, 6 * (planes - 2))):
+        hidden = call(
+            functools.partial(side_kernel, axis),
+            hidden_shape,
+            (own, halo, taps1, b1, hidden),
+            row_flops * count_rows,
+            12,
+            {4: 0},
+        )
 
     def image_shape(width):
         return jax.ShapeDtypeStruct((rows + -(-rows // width), width, lanes), F32)
@@ -309,7 +366,6 @@
     half = image_shape(chans // 2)
     _, send, keep = call(
         functools.partial(field_kernel, 2.0 / (planes * count), unit),
-        "field",
         (hidden_shape, half, half),
         (own, tiles, depths, corners, taps1, b1, taps2, b2, dens, hidden),
         row_flops * (36 + planes * rows),
@@ -320,12 +376,9 @@
         got = lax.ppermute(send, "depth", [(i, i ^ (1 << level)) for i in range(count)])
         if level < levels - 1:
             part = image_shape(send.shape[1] // 2)
-            send, keep = call(
-                functools.partial(merge_kernel, rows, level, unit), "merge", (part, part), (keep, got), 1 << 20, 4
-            )
+            send, keep = call(functools.partial(merge_kernel, rows, level, unit), (part, part), (keep, got), 1 << 20, 4)
     return call(
         functools.partial(last_kernel, rows, levels - 1),
-        "last",
         jax.ShapeDtypeStruct((unit, rows, lanes), F32),
         (keep, got),
         1 << 20,
@@ -335,6 +388,7 @@
 
 def solution(mesh):
     placed = (P(None, ("groups", "depth"), "tile", None), P(), P(), P(), P(), P())
+
     return jax.shard_map(
         body,
         mesh=mesh,

time: 37.7 us -> 35.4 us (0.939)
  the two profiles are of different devices: /device:TPU:20 before, /device:TPU:8 now
where the time goes in v2:
time: 35.4 us; the launch traced here: 35.2 us
  starting transfers between devices  15.3 us (43%)
  Pallas kernels  12.5 us (35%)
  waiting for transfers between devices  7.1 us (20%)
    pallas_call x8, Pallas kernels, call(): pl.pallas_call(kernel, out_shape=outs, in_specs=[pl.BlockSpec(memory_spac...  12.5 us
    ppermute x5, starting transfers between devices, swap(): return lax.ppermute(block, axis, partners(axis, far))  12.4 us
    ppermute x2, waiting for transfers between devices, body(): lax.ppermute(send, 'depth', [(i, i ^ 1 << level) for i in range(count)])  4.46 us
    ppermute x5, waiting for transfers between devices, swap(): return lax.ppermute(block, axis, partners(axis, far))  2.63 us
    ppermute x2, starting transfers between devices, body(): lax.ppermute(send, 'depth', [(i, i ^ 1 << level) for i in range(count)])  1.56 us
    ppermute x2, starting transfers between devices, swap_corner(): return lax.ppermute(block, ('tile', 'depth'), pairs)  1.34 us
  transfers between devices with their start and end apart: 9, of which 3 were waited for; matrix products, arithmetic and copies ran while one was open for 0% of the time, Pallas kernels for 15%

profile of v2, /device:TPU:8, one launch (start us, length us, event | category | flops | bytes accessed | tf_op | source)
XLA Modules:
  0.0 35.2 jit_solution(10487000219265739405)
XLA Ops:
  0.0 1.8 %shard_map.64 = (bf16[8,8,64,128]{3,2,1,0:T(8,128)(2,1)S(1)}, bf16[8,3,64,128]{3,2,1,0:T(8,128)(2,1)S(1)}, bf16[8,3,64,128]{3,2,1,0:T(8,128)(2,1)S(1)}, bf16[3,8...) custom-call(bf16[64,8,8,128]{3,2,1,0:T(8,128)(2,1)} %volume_ref.1, ...), custom_call_target="tpu_custom_call" | custom-call | flops 1048576 | bytes 1048576 | tf_op jit(solution)/shard_map/pallas_call | solution.py:293
  1.8 0.7 %collective-permute-start.5 = (bf16[3,3,64,128]{3,2,1,0:T(8,128)(2,1)S(1)}, bf16[3,3,64,128]{3,2,1,0:T(8,128)(2,1)S(1)}, u32[]{:S(2)}, u32[]{:S(2)}) collective-permute-start(bf16[3,3,64,128]{3,2,1,0:T(8,128)(2,1)S(1)} %get-tuple-element.33), channel_id=1, source_target_pairs={{1,6},{2,5},{5,2},{6,1},{9,14},{10,13},{13,10},{14,9},{17,22},{18,... | collective-permute-start | bytes 442376 | tf_op jit(solution)/shard_map/ppermute | solution.py:39
  2.5 0.1 collective-permute-start
  2.6 5.0 %collective-permute-start.1 = (bf16[8,3,64,128]{3,2,1,0:T(8,128)(2,1)S(1)}, bf16[8,3,64,128]{3,2,1,0:T(8,128)(2,1)S(1)}, u32[]{:S(2)}, u32[]{:S(2)}) collective-permute-start(bf16[8,3,64,128]{3,2,1,0:T(8,128)(2,1)S(1)} %get-tuple-element.28), channel_id=1, source_target_pairs={{4,8},{8,4},{5,9},{9,5},{6,10},{10,6},{7,11},{11,7},{20,24},{24,20... | collective-permute-start | bytes 1179656 | tf_op jit(solution)/shard_map/ppermute | solution.py:31
  7.6 2.2 %collective-permute-start.2 = (bf16[3,8,64,128]{3,2,1,0:T(8,128)(2,1)S(1)}, bf16[3,8,64,128]{3,2,1,0:T(8,128)(2,1)S(1)}, u32[]{:S(2)}, u32[]{:S(2)}) collective-permute-start(bf16[3,8,64,128]{3,2,1,0:T(8,128)(2,1)S(1)} %get-tuple-element.30), channel_id=1, source_target_pairs={{0,1},{1,0},{2,3},{3,2},{4,5},{5,4},{6,7},{7,6},{8,9},{9,8},{10,11... | collective-permute-start | bytes 1179656 | tf_op jit(solution)/shard_map/ppermute | solution.py:31
  9.9 0.7 %collective-permute-start.3 = (bf16[3,8,64,128]{3,2,1,0:T(8,128)(2,1)S(1)}, bf16[3,8,64,128]{3,2,1,0:T(8,128)(2,1)S(1)}, u32[]{:S(2)}, u32[]{:S(2)}) collective-permute-start(bf16[3,8,64,128]{3,2,1,0:T(8,128)(2,1)S(1)} %get-tuple-element.31), channel_id=1, source_target_pairs={{1,2},{2,1},{5,6},{6,5},{9,10},{10,9},{13,14},{14,13},{17,18},{18,... | collective-permute-start | bytes 1179656 | tf_op jit(solution)/shard_map/ppermute | solution.py:31
  10.6 0.0 collective-permute-done.5
  10.6 0.7 %collective-permute-start.6 = (bf16[3,3,64,128]{3,2,1,0:T(8,128)(2,1)S(1)}, bf16[3,3,64,128]{3,2,1,0:T(8,128)(2,1)S(1)}, u32[]{:S(2)}, u32[]{:S(2)}) collective-permute-start(bf16[3,3,64,128]{3,2,1,0:T(8,128)(2,1)S(1)} %get-tuple-element.34), channel_id=1, source_target_pairs={{5,10},{6,9},{9,6},{10,5},{21,26},{22,25},{25,22},{26,21}} | collective-permute-start | bytes 442376 | tf_op jit(solution)/shard_map/ppermute | solution.py:39
  11.2 1.7 %shard_map.66 = (bf16[12,12,64,128]{3,2,1,0:T(8,128)(2,1)S(1)}, bf16[192,576]{1,0:T(8,128)(2,1)S(1)}, bf16[192,576]{1,0:T(8,128)(2,1)S(1)}) custom-call(bf16[8,8,64,128]{3,2,1,0:T(8,128)(2,1)S(1)} %get-tuple-element.26.own_ref, bf16[27,64,64]{2,1,0:T(8,128)(2,1)S(1)} %get-tuple-element.35.w1_ref, f32[1,64]{1,0:T(1,128)S(1)} %get-tuple-element.36.b1_ref, ...), custom_call_target="tpu_custom_call" | custom-call | flops 1019215872 | bytes 1048576 | tf_op jit(solution)/shard_map/pallas_call | solution.py:293
  13.0 0.0 collective-permute-done.6
  13.0 0.0 collective-permute-done.near_ref
  13.1 2.6 %collective-permute-done.1.far_ref = bf16[8,3,64,128]{3,2,1,0:T(8,128)(2,1)S(1)} collective-permute-done((bf16[8,3,64,128]{3,2,1,0:T(8,128)(2,1)S(1)}, bf16[8,3,64,128]{3,2,1,0:T(8,128)(2,1)S(1)}, u32[]{:S(2)}, u32[]{:S(2)}) %collective-permute-start.1) | collective-permute-done | bytes 393248 | tf_op jit(solution)/shard_map/ppermute | solution.py:31
  15.7 0.1 shard_map.65
  15.8 4.4 %collective-permute-start.4 = (bf16[2,3,3,64,128]{4,3,2,1,0:T(8,128)(2,1)S(1)}, bf16[2,3,3,64,128]{4,3,2,1,0:T(8,128)(2,1)S(1)}, u32[]{:S(2)}, u32[]{:S(2)}) collective-permute-start(bf16[2,3,3,64,128]{4,3,2,1,0:T(8,128)(2,1)S(1)} %get-tuple-element.32), channel_id=1, source_target_pairs={{0,1},{1,0},{2,3},{3,2},{4,5},{5,4},{6,7},{7,6},{8,9},{9,8},{10,11... | collective-permute-start | bytes 884744 | tf_op jit(solution)/shard_map/ppermute | solution.py:31
  20.2 0.0 collective-permute-done.2
  20.2 0.0 collective-permute-done.3
  20.2 0.1 pad_maximum_fusion.halo_ref.depths_ref
  20.3 1.7 %shard_map.67.given_ref = bf16[12,12,64,128]{3,2,1,0:T(8,128)(2,1)S(1)} custom-call(bf16[8,8,64,128]{3,2,1,0:T(8,128)(2,1)S(1)} %get-tuple-element.26.own_ref, bf16[2,3,8,64,128]{4,3,2,1,0:T(8,128)(2,1)S(1)} %pad_maximum_fusion.halo_ref.depths_ref, bf16[192,576]{1,0:T(8,128)(2,1)S(1)} %get-tuple-element.38.taps_ref.taps1_ref, ...), custom_call_target="tpu_custom_call", output_to_operand_aliasing={{}: (4, {})} | custom-call | flops 1019215872 | bytes 1048576 | tf_op jit(solution)/shard_map/pallas_call | solution.py:293
  21.9 1.7 %shard_map.68.given_ref = bf16[12,12,64,128]{3,2,1,0:T(8,128)(2,1)S(1)} custom-call(bf16[8,8,64,128]{3,2,1,0:T(8,128)(2,1)S(1)} %get-tuple-element.26.own_ref, bf16[2,8,3,64,128]{4,3,2,1,0:T(8,128)(2,1)S(1)} %get-tuple-element.29.halo_ref.tiles_ref, bf16[192,576]{1,0:T(8,128)(2,1)S(1)} %get-tuple-element.38.taps_ref.taps1_ref, ...), custom_call_target="tpu_custom_call", output_to_operand_aliasing={{}: (4, {})} | custom-call | flops 1019215872 | bytes 1048576 | tf_op jit(solution)/shard_map/pallas_call | solution.py:293
  23.6 0.0 collective-permute-done.4
  23.6 0.1 pad_maximum_fusion.1.corners_ref
  23.7 4.8 %shard_map.69 = (bf16[12,12,64,128]{3,2,1,0:T(8,128)(2,1)S(1)}, f32[9,32,128]{2,1,0:T(8,128)S(1)}, f32[9,32,128]{2,1,0:T(8,128)S(1)}) custom-call(bf16[8,8,64,128]{3,2,1,0:T(8,128)(2,1)S(1)} %get-tuple-element.26.own_ref, bf16[2,8,3,64,128]{4,3,2,1,0:T(8,128)(2,1)S(1)} %get-tuple-element.29.halo_ref.tiles_ref, ...), custom_call_target="tpu_custom_call", output_to_operand_aliasing={{0}: (9, {})} | custom-call | flops 2831155200 | bytes 1048576 | tf_op jit(solution)/shard_map/pallas_call | solution.py:293
  28.5 0.4 %collective-permute-start.7 = (f32[9,32,128]{2,1,0:T(8,128)S(1)}, f32[9,32,128]{2,1,0:T(8,128)S(1)}, u32[]{:S(2)}, u32[]{:S(2)}) collective-permute-start(f32[9,32,128]{2,1,0:T(8,128)S(1)} %get-tuple-element.44), channel_id=1, source_target_pairs={{0,1},{1,0},{2,3},{3,2},{4,5},{5,4},{6,7},{7,6},{8,9},{9,8},{10,11... | collective-permute-start | bytes 442376 | tf_op jit(solution)/shard_map/ppermute | solution.py:376
  28.9 1.0 %collective-permute-done.7.other_ref = f32[9,32,128]{2,1,0:T(8,128)S(1)} collective-permute-done((f32[9,32,128]{2,1,0:T(8,128)S(1)}, f32[9,32,128]{2,1,0:T(8,128)S(1)}, u32[]{:S(2)}, u32[]{:S(2)}) %collective-permute-start.7) | collective-permute-done | bytes 147488 | tf_op jit(solution)/shard_map/ppermute | solution.py:376
  29.9 1.2 %collective-permute-start.8 = (f32[9,16,128]{2,1,0:T(8,128)S(1)}, f32[9,16,128]{2,1,0:T(8,128)S(1)}, u32[]{:S(2)}, u32[]{:S(2)}) collective-permute-start(f32[9,16,128]{2,1,0:T(8,128)S(1)} %get-tuple-element.46), channel_id=1, source_target_pairs={{0,2},{1,3},{2,0},{3,1},{4,6},{5,7},{6,4},{7,5},{8,10},{9,11},{10,... | collective-permute-start | bytes 221192 | tf_op jit(solution)/shard_map/ppermute | solution.py:376
  31.1 3.4 %collective-permute-done.8.other_ref = f32[9,16,128]{2,1,0:T(8,128)S(1)} collective-permute-done((f32[9,16,128]{2,1,0:T(8,128)S(1)}, f32[9,16,128]{2,1,0:T(8,128)S(1)}, u32[]{:S(2)}, u32[]{:S(2)}) %collective-permute-start.8) | collective-permute-done | bytes 73760 | tf_op jit(solution)/shard_map/ppermute | solution.py:376
  34.5 0.7 %shard_map.71 = f32[16,8,128]{2,1,0:T(8,128)} custom-call(f32[9,16,128]{2,1,0:T(8,128)S(1)} %get-tuple-element.45.mine_ref, f32[9,16,128]{2,1,0:T(8,128)S(1)} %collective-permute-done.8.other_ref), custom_call_target="tpu_custom_call" | custom-call | flops 1048576 | bytes 1048576 | tf_op jit(solution)/shard_map/pallas_call | solution.py:293
  (2 shorter events, 0.1 us)
Async XLA Ops:
  1.8 8.7 %collective-permute-start.5 = (bf16[3,3,64,128]{3,2,1,0:T(8,128)(2,1)S(1)}, bf16[3,3,64,128]{3,2,1,0:T(8,128)(2,1)S(1)}, u32[]{:S(2)}, u32[]{:S(2)}) collective-permute-start(bf16[3,3,64,128]{3,2,1,0:T(8,128)(2,1)S(1)} %get-tuple-element.33), channel_id=1, source_target_pairs={{1,6},{2,5},{5,2},{6,1},{9,14},{10,13},{13,10},{14,9},{17,22},{18,... | collective-permute-start | bytes 442376 | tf_op jit(solution)/shard_map/ppermute | solution.py:39
  2.5 10.6 %collective-permute-start = (bf16[8,3,64,128]{3,2,1,0:T(8,128)(2,1)S(1)}, bf16[8,3,64,128]{3,2,1,0:T(8,128)(2,1)S(1)}, u32[]{:S(2)}, u32[]{:S(2)}) collective-permute-start(bf16[8,3,64,128]{3,2,1,0:T(8,128)(2,1)S(1)} %get-tuple-element.27), channel_id=1, source_target_pairs={{0,4},{4,0},{8,12},{12,8},{1,5},{5,1},{9,13},{13,9},{2,6},{6,2},{1... | collective-permute-start | bytes 1179656 | tf_op jit(solution)/shard_map/ppermute | solution.py:31
  2.6 13.1 %collective-permute-start.1 = (bf16[8,3,64,128]{3,2,1,0:T(8,128)(2,1)S(1)}, bf16[8,3,64,128]{3,2,1,0:T(8,128)(2,1)S(1)}, u32[]{:S(2)}, u32[]{:S(2)}) collective-permute-start(bf16[8,3,64,128]{3,2,1,0:T(8,128)(2,1)S(1)} %get-tuple-element.28), channel_id=1, source_target_pairs={{4,8},{8,4},{5,9},{9,5},{6,10},{10,6},{7,11},{11,7},{20,24},{24,20... | collective-permute-start | bytes 1179656 | tf_op jit(solution)/shard_map/ppermute | solution.py:31
  7.6 12.5 %collective-permute-start.2 = (bf16[3,8,64,128]{3,2,1,0:T(8,128)(2,1)S(1)}, bf16[3,8,64,128]{3,2,1,0:T(8,128)(2,1)S(1)}, u32[]{:S(2)}, u32[]{:S(2)}) collective-permute-start(bf16[3,8,64,128]{3,2,1,0:T(8,128)(2,1)S(1)} %get-tuple-element.30), channel_id=1, source_target_pairs={{0,1},{1,0},{2,3},{3,2},{4,5},{5,4},{6,7},{7,6},{8,9},{9,8},{10,11... | collective-permute-start | bytes 1179656 | tf_op jit(solution)/shard_map/ppermute | solution.py:31
  9.9 10.3 %collective-permute-start.3 = (bf16[3,8,64,128]{3,2,1,0:T(8,128)(2,1)S(1)}, bf16[3,8,64,128]{3,2,1,0:T(8,128)(2,1)S(1)}, u32[]{:S(2)}, u32[]{:S(2)}) collective-permute-start(bf16[3,8,64,128]{3,2,1,0:T(8,128)(2,1)S(1)} %get-tuple-element.31), channel_id=1, source_target_pairs={{1,2},{2,1},{5,6},{6,5},{9,10},{10,9},{13,14},{14,13},{17,18},{18,... | collective-permute-start | bytes 1179656 | tf_op jit(solution)/shard_map/ppermute | solution.py:31
  10.6 2.4 %collective-permute-start.6 = (bf16[3,3,64,128]{3,2,1,0:T(8,128)(2,1)S(1)}, bf16[3,3,64,128]{3,2,1,0:T(8,128)(2,1)S(1)}, u32[]{:S(2)}, u32[]{:S(2)}) collective-permute-start(bf16[3,3,64,128]{3,2,1,0:T(8,128)(2,1)S(1)} %get-tuple-element.34), channel_id=1, source_target_pairs={{5,10},{6,9},{9,6},{10,5},{21,26},{22,25},{25,22},{26,21}} | collective-permute-start | bytes 442376 | tf_op jit(solution)/shard_map/ppermute | solution.py:39
  15.8 7.9 %collective-permute-start.4 = (bf16[2,3,3,64,128]{4,3,2,1,0:T(8,128)(2,1)S(1)}, bf16[2,3,3,64,128]{4,3,2,1,0:T(8,128)(2,1)S(1)}, u32[]{:S(2)}, u32[]{:S(2)}) collective-permute-start(bf16[2,3,3,64,128]{4,3,2,1,0:T(8,128)(2,1)S(1)} %get-tuple-element.32), channel_id=1, source_target_pairs={{0,1},{1,0},{2,3},{3,2},{4,5},{5,4},{6,7},{7,6},{8,9},{9,8},{10,11... | collective-permute-start | bytes 884744 | tf_op jit(solution)/shard_map/ppermute | solution.py:31
  28.5 1.4 %collective-permute-start.7 = (f32[9,32,128]{2,1,0:T(8,128)S(1)}, f32[9,32,128]{2,1,0:T(8,128)S(1)}, u32[]{:S(2)}, u32[]{:S(2)}) collective-permute-start(f32[9,32,128]{2,1,0:T(8,128)S(1)} %get-tuple-element.44), channel_id=1, source_target_pairs={{0,1},{1,0},{2,3},{3,2},{4,5},{5,4},{6,7},{7,6},{8,9},{9,8},{10,11... | collective-permute-start | bytes 442376 | tf_op jit(solution)/shard_map/ppermute | solution.py:376
  29.9 4.6 %collective-permute-start.8 = (f32[9,16,128]{2,1,0:T(8,128)S(1)}, f32[9,16,128]{2,1,0:T(8,128)S(1)}, u32[]{:S(2)}, u32[]{:S(2)}) collective-permute-start(f32[9,16,128]{2,1,0:T(8,128)S(1)} %get-tuple-element.46), channel_id=1, source_target_pairs={{0,2},{1,3},{2,0},{3,1},{4,6},{5,7},{6,4},{7,5},{8,10},{9,11},{10,... | collective-permute-start | bytes 221192 | tf_op jit(solution)/shard_map/ppermute | solution.py:376

commit v3 on v2

--- a/solution.py
+++ b/solution.py
@@ -151,7 +151,43 @@
     return [[(z, x), (z, x + 1)] for x in range(HALO, rows + 1, 2) for z in edge_list(planes)]
 
 
-def side_kernel(axis, own_ref, halo_ref, taps_ref, b1_ref, given_ref, hidden_ref):
+def depth_kernel(own_ref, halo_ref, taps_ref, b1_ref, given_ref, hidden_ref):
+    planes, rows, chans, lanes = own_ref.shape
+    put_sides("depth", own_ref, halo_ref, taps_ref, b1_ref, hidden_ref)
+    index = lax.axis_index("depth")
+    inside = rows - 2
+
+    @pl.when(index == 0)
+    def _():
+        hidden_ref[0:2, HALO : rows + 1] = jnp.zeros((2, inside, chans, lanes), BF16)
+
+    @pl.when(index == lax.axis_size("depth") - 1)
+    def _():
+        hidden_ref[planes + 2 :, HALO : rows + 1] = jnp.zeros((2, inside, chans, lanes), BF16)
+
+
+def tile_kernel(
+    tau_scale,
+    own_ref,
+    halo_ref,
+    taps1_ref,
+    b1_ref,
+    taps2_ref,
+    b2_ref,
+    dens_ref,
+    given_ref,
+    hidden_ref,
+    middle_ref,
+):
+    planes, rows, chans, _ = own_ref.shape
+    put_sides("tile", own_ref, halo_ref, taps1_ref, b1_ref, hidden_ref)
+    pieces = render(tau_scale, planes, middle_rows(rows), taps2_ref, b2_ref, dens_ref, hidden_ref)
+    for at, (_, image, depth) in enumerate(pieces):
+        middle_ref[at, :chans] = image
+        middle_ref[at, chans : chans + 1] = depth
+
+
+def put_sides(axis, own_ref, halo_ref, taps_ref, b1_ref, hidden_ref):
     planes, rows, chans, lanes = own_ref.shape
     odd = lax.axis_index(axis) % 2
     bias = column_of(b1_ref, lanes)
@@ -182,6 +218,31 @@
     for ref, value in ((send_ref, send), (keep_ref, keep)):
         ref[row] = value
         ref[rows + row // width, pl.ds(row % width, 1)] = depth
+
+
+def middle_rows(rows):
+    return list(range(HALO, rows - HALO))
+
+
+def render(tau_scale, planes, rows, taps_ref, b2_ref, dens_ref, hidden_ref):
+    chans, lanes = hidden_ref.shape[2:]
+    bias, dens = column_of(b2_ref, lanes), column_of(dens_ref, lanes)
+    for start in range(0, len(rows), 2):
+        pair = rows[start : start + 2]
+        image = [jnp.zeros((chans, lanes), F32) for _ in pair]
+        depth = [jnp.zeros((1, lanes), F32) for _ in pair]
+        for plane in range(planes):
+            spots = [(plane, row) for row in pair]
+            sums = conv_spots(taps_ref, lambda z, x: hidden_ref[z, x], spots, 2, chans, lanes)
+            for r, value in enumerate(sums):
+                feat = silu(value + bias).astype(BF16).astype(F32)
+                logit = jnp.sum(feat * dens, axis=0, keepdims=True)
+                tau = jax.nn.softplus(logit) * tau_scale
+                half = jnp.tanh(0.5 * tau)
+                weight = (jnp.exp(-depth[r]) * (2.0 * half / (1.0 + half))).astype(BF16).astype(F32)
+                image[r] = image[r] + weight * feat
+                depth[r] = depth[r] + tau
+        yield from zip(pair, image, depth)
 
 
 def field_kernel(
@@ -197,6 +258,7 @@
     b2_ref,
     dens_ref,
     given_ref,
+    middle_ref,
     hidden_ref,
     send_ref,
     keep_ref,
@@ -243,26 +305,11 @@
     def _():
         hidden_ref[planes + 2 :] = jnp.zeros((2, rows + 4, chans, lanes), BF16)
 
-    bias2 = column_of(b2_ref, lanes)
-    dens = column_of(dens_ref, lanes)
-
-    for row in range(0, rows, 2):
-        image = [jnp.zeros((chans, lanes), F32) for _ in range(2)]
-        depth = [jnp.zeros((1, lanes), F32) for _ in range(2)]
-        for plane in range(planes):
-            sums = conv_spots(
-                taps2_ref, lambda z, x: hidden_ref[z, x], [(plane, row), (plane, row + 1)], 2, chans, lanes
-            )
-            for r in range(2):
-                feat = silu(sums[r] + bias2).astype(BF16).astype(F32)
-                logit = jnp.sum(feat * dens, axis=0, keepdims=True)
-                tau = jax.nn.softplus(logit) * tau_scale
-                half = jnp.tanh(0.5 * tau)
-                weight = (jnp.exp(-depth[r]) * (2.0 * half / (1.0 + half))).astype(BF16).astype(F32)
-                image[r] = image[r] + weight * feat
-                depth[r] = depth[r] + tau
-        for r in range(2):
-            put_image(row + r, rows, image[r], depth[r], depth_odd, unit, send_ref, keep_ref)
+    for at, row in enumerate(middle_rows(rows)):
+        put_image(row, rows, middle_ref[at, :chans], middle_ref[at, chans : chans + 1], depth_odd, unit, send_ref, keep_ref)
+    outer = [row for row in range(rows) if row not in middle_rows(rows)]
+    for row, image, depth in render(tau_scale, planes, outer, taps2_ref, b2_ref, dens_ref, hidden_ref):
+        put_image(row, rows, image, depth, depth_odd, unit, send_ref, keep_ref)
 
 
 def merge_rows(rows, mine_ref, other_ref, bit):
@@ -350,25 +397,27 @@
     hidden, taps1, taps2 = call(
         inner_kernel, (hidden_shape, taps_shape, taps_shape), (own, w1, b1, w2), row_flops * inner, 12
     )
-    for axis, halo, count_rows in (("depth", depths, 6 * (rows - 2)), ("tile", tiles, 6 * (planes - 2))):
-        hidden = call(
-            functools.partial(side_kernel, axis),
-            hidden_shape,
-            (own, halo, taps1, b1, hidden),
-            row_flops * count_rows,
-            12,
-            {4: 0},
-        )
+    tau_scale = 2.0 / (planes * count)
+    hidden = call(depth_kernel, hidden_shape, (own, depths, taps1, b1, hidden), row_flops * 6 * (rows - 2), 12, {4: 0})
+    mids = len(middle_rows(rows))
+    hidden, middle = call(
+        functools.partial(tile_kernel, tau_scale),
+        (hidden_shape, jax.ShapeDtypeStruct((mids, chans + 8, lanes), F32)),
+        (own, tiles, taps1, b1, taps2, b2, dens, hidden),
+        row_flops * (6 * (planes - 2) + mids * planes),
+        12,
+        {7: 0},
+    )
 
     def image_shape(width):
         return jax.ShapeDtypeStruct((rows + -(-rows // width), width, lanes), F32)
 
     half = image_shape(chans // 2)
     _, send, keep = call(
-        functools.partial(field_kernel, 2.0 / (planes * count), unit),
+        functools.partial(field_kernel, tau_scale, unit),
         (hidden_shape, half, half),
-        (own, tiles, depths, corners, taps1, b1, taps2, b2, dens, hidden),
-        row_flops * (36 + planes * rows),
+        (own, tiles, depths, corners, taps1, b1, taps2, b2, dens, hidden, middle),
+        row_flops * (36 + planes * (rows - mids)),
         12,
         {9: 0},
     )

time: 35.4 us -> 35.5 us (level)
  the two profiles are of different devices: /device:TPU:8 before, /device:TPU:12 now
where the time goes in v3:
time: 35.5 us; the launch traced here: 35.3 us
  starting transfers between devices  15.3 us (43%)
  Pallas kernels  12.5 us (35%)
  waiting for transfers between devices  7.08 us (20%)
    pallas_call x8, Pallas kernels, call(): pl.pallas_call(kernel, out_shape=outs, in_specs=[pl.BlockSpec(memory_spac...  12.5 us
    ppermute x5, starting transfers between devices, swap(): return lax.ppermute(block, axis, partners(axis, far))  12.4 us
    ppermute x2, waiting for transfers between devices, body(): lax.ppermute(send, 'depth', [(i, i ^ 1 << level) for i in range(count)])  4.44 us
    ppermute x5, waiting for transfers between devices, swap(): return lax.ppermute(block, axis, partners(axis, far))  2.63 us
    ppermute x2, starting transfers between devices, body(): lax.ppermute(send, 'depth', [(i, i ^ 1 << level) for i in range(count)])  1.56 us
    ppermute x2, starting transfers between devices, swap_corner(): return lax.ppermute(block, ('tile', 'depth'), pairs)  1.34 us
  transfers between devices with their start and end apart: 9, of which 3 were waited for; matrix products, arithmetic and copies ran while one was open for 0% of the time, Pallas kernels for 17%

profile of v3, /device:TPU:12, one launch (start us, length us, event | category | flops | bytes accessed | tf_op | source)
XLA Modules:
  0.0 35.3 jit_solution(6471109643007008083)
XLA Ops:
  0.0 1.8 %shard_map.64 = (bf16[8,8,64,128]{3,2,1,0:T(8,128)(2,1)S(1)}, bf16[8,3,64,128]{3,2,1,0:T(8,128)(2,1)S(1)}, bf16[8,3,64,128]{3,2,1,0:T(8,128)(2,1)S(1)}, bf16[3,8...) custom-call(bf16[64,8,8,128]{3,2,1,0:T(8,128)(2,1)} %volume_ref.1, ...), custom_call_target="tpu_custom_call" | custom-call | flops 1048576 | bytes 1048576 | tf_op jit(solution)/shard_map/pallas_call | solution.py:340
  1.8 0.7 %collective-permute-start.5 = (bf16[3,3,64,128]{3,2,1,0:T(8,128)(2,1)S(1)}, bf16[3,3,64,128]{3,2,1,0:T(8,128)(2,1)S(1)}, u32[]{:S(2)}, u32[]{:S(2)}) collective-permute-start(bf16[3,3,64,128]{3,2,1,0:T(8,128)(2,1)S(1)} %get-tuple-element.35), channel_id=1, source_target_pairs={{1,6},{2,5},{5,2},{6,1},{9,14},{10,13},{13,10},{14,9},{17,22},{18,... | collective-permute-start | bytes 442376 | tf_op jit(solution)/shard_map/ppermute | solution.py:39
  2.5 0.5 %collective-permute-start = (bf16[8,3,64,128]{3,2,1,0:T(8,128)(2,1)S(1)}, bf16[8,3,64,128]{3,2,1,0:T(8,128)(2,1)S(1)}, u32[]{:S(2)}, u32[]{:S(2)}) collective-permute-start(bf16[8,3,64,128]{3,2,1,0:T(8,128)(2,1)S(1)} %get-tuple-element.29), channel_id=1, source_target_pairs={{0,4},{4,0},{8,12},{12,8},{1,5},{5,1},{9,13},{13,9},{2,6},{6,2},{1... | collective-permute-start | bytes 1179656 | tf_op jit(solution)/shard_map/ppermute | solution.py:31
  3.0 4.6 %collective-permute-start.1 = (bf16[8,3,64,128]{3,2,1,0:T(8,128)(2,1)S(1)}, bf16[8,3,64,128]{3,2,1,0:T(8,128)(2,1)S(1)}, u32[]{:S(2)}, u32[]{:S(2)}) collective-permute-start(bf16[8,3,64,128]{3,2,1,0:T(8,128)(2,1)S(1)} %get-tuple-element.30), channel_id=1, source_target_pairs={{4,8},{8,4},{5,9},{9,5},{6,10},{10,6},{7,11},{11,7},{20,24},{24,20... | collective-permute-start | bytes 1179656 | tf_op jit(solution)/shard_map/ppermute | solution.py:31
  7.6 2.2 %collective-permute-start.2 = (bf16[3,8,64,128]{3,2,1,0:T(8,128)(2,1)S(1)}, bf16[3,8,64,128]{3,2,1,0:T(8,128)(2,1)S(1)}, u32[]{:S(2)}, u32[]{:S(2)}) collective-permute-start(bf16[3,8,64,128]{3,2,1,0:T(8,128)(2,1)S(1)} %get-tuple-element.32), channel_id=1, source_target_pairs={{0,1},{1,0},{2,3},{3,2},{4,5},{5,4},{6,7},{7,6},{8,9},{9,8},{10,11... | collective-permute-start | bytes 1179656 | tf_op jit(solution)/shard_map/ppermute | solution.py:31
  9.9 0.7 %collective-permute-start.3 = (bf16[3,8,64,128]{3,2,1,0:T(8,128)(2,1)S(1)}, bf16[3,8,64,128]{3,2,1,0:T(8,128)(2,1)S(1)}, u32[]{:S(2)}, u32[]{:S(2)}) collective-permute-start(bf16[3,8,64,128]{3,2,1,0:T(8,128)(2,1)S(1)} %get-tuple-element.33), channel_id=1, source_target_pairs={{1,2},{2,1},{5,6},{6,5},{9,10},{10,9},{13,14},{14,13},{17,18},{18,... | collective-permute-start | bytes 1179656 | tf_op jit(solution)/shard_map/ppermute | solution.py:31
  10.6 0.0 collective-permute-done.5
  10.6 0.7 %collective-permute-start.6 = (bf16[3,3,64,128]{3,2,1,0:T(8,128)(2,1)S(1)}, bf16[3,3,64,128]{3,2,1,0:T(8,128)(2,1)S(1)}, u32[]{:S(2)}, u32[]{:S(2)}) collective-permute-start(bf16[3,3,64,128]{3,2,1,0:T(8,128)(2,1)S(1)} %get-tuple-element.36), channel_id=1, source_target_pairs={{5,10},{6,9},{9,6},{10,5},{21,26},{22,25},{25,22},{26,21}} | collective-permute-start | bytes 442376 | tf_op jit(solution)/shard_map/ppermute | solution.py:39
  11.2 1.7 %shard_map.66 = (bf16[12,12,64,128]{3,2,1,0:T(8,128)(2,1)S(1)}, bf16[192,576]{1,0:T(8,128)(2,1)S(1)}, bf16[192,576]{1,0:T(8,128)(2,1)S(1)}) custom-call(bf16[8,8,64,128]{3,2,1,0:T(8,128)(2,1)S(1)} %get-tuple-element.28.own_ref, bf16[27,64,64]{2,1,0:T(8,128)(2,1)S(1)} %get-tuple-element.37.w1_ref, f32[1,64]{1,0:T(1,128)S(1)} %get-tuple-element.38.b1_ref, ...), custom_call_target="tpu_custom_call" | custom-call | flops 1019215872 | bytes 1048576 | tf_op jit(solution)/shard_map/pallas_call | solution.py:340
  13.0 0.0 collective-permute-done.6
  13.0 0.0 collective-permute-done.near_ref
  13.1 2.6 %collective-permute-done.1.far_ref = bf16[8,3,64,128]{3,2,1,0:T(8,128)(2,1)S(1)} collective-permute-done((bf16[8,3,64,128]{3,2,1,0:T(8,128)(2,1)S(1)}, bf16[8,3,64,128]{3,2,1,0:T(8,128)(2,1)S(1)}, u32[]{:S(2)}, u32[]{:S(2)}) %collective-permute-start.1) | collective-permute-done | bytes 393248 | tf_op jit(solution)/shard_map/ppermute | solution.py:31
  15.7 0.1 shard_map.65
  15.8 4.4 %collective-permute-start.4 = (bf16[2,3,3,64,128]{4,3,2,1,0:T(8,128)(2,1)S(1)}, bf16[2,3,3,64,128]{4,3,2,1,0:T(8,128)(2,1)S(1)}, u32[]{:S(2)}, u32[]{:S(2)}) collective-permute-start(bf16[2,3,3,64,128]{4,3,2,1,0:T(8,128)(2,1)S(1)} %get-tuple-element.34), channel_id=1, source_target_pairs={{0,1},{1,0},{2,3},{3,2},{4,5},{5,4},{6,7},{7,6},{8,9},{9,8},{10,11... | collective-permute-start | bytes 884744 | tf_op jit(solution)/shard_map/ppermute | solution.py:31
  20.2 0.0 collective-permute-done.2
  20.2 0.0 collective-permute-done.3
  20.2 0.1 pad_maximum_fusion.halo_ref.depths_ref
  20.3 1.7 %shard_map.67.given_ref = bf16[12,12,64,128]{3,2,1,0:T(8,128)(2,1)S(1)} custom-call(bf16[8,8,64,128]{3,2,1,0:T(8,128)(2,1)S(1)} %get-tuple-element.28.own_ref, bf16[2,3,8,64,128]{4,3,2,1,0:T(8,128)(2,1)S(1)} %pad_maximum_fusion.halo_ref.depths_ref, bf16[192,576]{1,0:T(8,128)(2,1)S(1)} %get-tuple-element.40.taps_ref.taps1_ref, ...), custom_call_target="tpu_custom_call", output_to_operand_aliasing={{}: (4, {})} | custom-call | flops 1019215872 | bytes 1048576 | tf_op jit(solution)/shard_map/pallas_call | solution.py:340
  22.0 2.4 %shard_map.68 = (bf16[12,12,64,128]{3,2,1,0:T(8,128)(2,1)S(1)}, f32[2,72,128]{2,1,0:T(8,128)S(1)}) custom-call(bf16[8,8,64,128]{3,2,1,0:T(8,128)(2,1)S(1)} %get-tuple-element.28.own_ref, bf16[2,8,3,64,128]{4,3,2,1,0:T(8,128)(2,1)S(1)} %get-tuple-element.31.halo_ref.tiles_ref, ...), custom_call_target="tpu_custom_call", output_to_operand_aliasing={{0}: (7, {})} | custom-call | flops 1472200704 | bytes 1048576 | tf_op jit(solution)/shard_map/pallas_call | solution.py:340
  24.4 0.0 collective-permute-done.4
  24.4 0.1 pad_maximum_fusion.1.corners_ref
  24.4 4.1 %shard_map.69 = (bf16[12,12,64,128]{3,2,1,0:T(8,128)(2,1)S(1)}, f32[9,32,128]{2,1,0:T(8,128)S(1)}, f32[9,32,128]{2,1,0:T(8,128)S(1)}) custom-call(bf16[8,8,64,128]{3,2,1,0:T(8,128)(2,1)S(1)} %get-tuple-element.28.own_ref, bf16[2,8,3,64,128]{4,3,2,1,0:T(8,128)(2,1)S(1)} %get-tuple-element.31.halo_ref.tiles_ref, ...), custom_call_target="tpu_custom_call", output_to_operand_aliasing={{0}: (9, {})} | custom-call | flops 2378170368 | bytes 1048576 | tf_op jit(solution)/shard_map/pallas_call | solution.py:340
  28.5 0.4 %collective-permute-start.7 = (f32[9,32,128]{2,1,0:T(8,128)S(1)}, f32[9,32,128]{2,1,0:T(8,128)S(1)}, u32[]{:S(2)}, u32[]{:S(2)}) collective-permute-start(f32[9,32,128]{2,1,0:T(8,128)S(1)} %get-tuple-element.48), channel_id=1, source_target_pairs={{0,1},{1,0},{2,3},{3,2},{4,5},{5,4},{6,7},{7,6},{8,9},{9,8},{10,11... | collective-permute-start | bytes 442376 | tf_op jit(solution)/shard_map/ppermute | solution.py:425
  28.9 1.0 %collective-permute-done.7.other_ref = f32[9,32,128]{2,1,0:T(8,128)S(1)} collective-permute-done((f32[9,32,128]{2,1,0:T(8,128)S(1)}, f32[9,32,128]{2,1,0:T(8,128)S(1)}, u32[]{:S(2)}, u32[]{:S(2)}) %collective-permute-start.7) | collective-permute-done | bytes 147488 | tf_op jit(solution)/shard_map/ppermute | solution.py:425
  30.0 1.2 %collective-permute-start.8 = (f32[9,16,128]{2,1,0:T(8,128)S(1)}, f32[9,16,128]{2,1,0:T(8,128)S(1)}, u32[]{:S(2)}, u32[]{:S(2)}) collective-permute-start(f32[9,16,128]{2,1,0:T(8,128)S(1)} %get-tuple-element.50), channel_id=1, source_target_pairs={{0,2},{1,3},{2,0},{3,1},{4,6},{5,7},{6,4},{7,5},{8,10},{9,11},{10,... | collective-permute-start | bytes 221192 | tf_op jit(solution)/shard_map/ppermute | solution.py:425
  31.2 3.4 %collective-permute-done.8.other_ref = f32[9,16,128]{2,1,0:T(8,128)S(1)} collective-permute-done((f32[9,16,128]{2,1,0:T(8,128)S(1)}, f32[9,16,128]{2,1,0:T(8,128)S(1)}, u32[]{:S(2)}, u32[]{:S(2)}) %collective-permute-start.8) | collective-permute-done | bytes 73760 | tf_op jit(solution)/shard_map/ppermute | solution.py:425
  34.6 0.7 %shard_map.71 = f32[16,8,128]{2,1,0:T(8,128)} custom-call(f32[9,16,128]{2,1,0:T(8,128)S(1)} %get-tuple-element.49.mine_ref, f32[9,16,128]{2,1,0:T(8,128)S(1)} %collective-permute-done.8.other_ref), custom_call_target="tpu_custom_call" | custom-call | flops 1048576 | bytes 1048576 | tf_op jit(solution)/shard_map/pallas_call | solution.py:340
  (2 shorter events, 0.1 us)
Async XLA Ops:
  1.8 8.7 %collective-permute-start.5 = (bf16[3,3,64,128]{3,2,1,0:T(8,128)(2,1)S(1)}, bf16[3,3,64,128]{3,2,1,0:T(8,128)(2,1)S(1)}, u32[]{:S(2)}, u32[]{:S(2)}) collective-permute-start(bf16[3,3,64,128]{3,2,1,0:T(8,128)(2,1)S(1)} %get-tuple-element.35), channel_id=1, source_target_pairs={{1,6},{2,5},{5,2},{6,1},{9,14},{10,13},{13,10},{14,9},{17,22},{18,... | collective-permute-start | bytes 442376 | tf_op jit(solution)/shard_map/ppermute | solution.py:39
  2.5 10.6 %collective-permute-start = (bf16[8,3,64,128]{3,2,1,0:T(8,128)(2,1)S(1)}, bf16[8,3,64,128]{3,2,1,0:T(8,128)(2,1)S(1)}, u32[]{:S(2)}, u32[]{:S(2)}) collective-permute-start(bf16[8,3,64,128]{3,2,1,0:T(8,128)(2,1)S(1)} %get-tuple-element.29), channel_id=1, source_target_pairs={{0,4},{4,0},{8,12},{12,8},{1,5},{5,1},{9,13},{13,9},{2,6},{6,2},{1... | collective-permute-start | bytes 1179656 | tf_op jit(solution)/shard_map/ppermute | solution.py:31
  3.0 12.6 %collective-permute-start.1 = (bf16[8,3,64,128]{3,2,1,0:T(8,128)(2,1)S(1)}, bf16[8,3,64,128]{3,2,1,0:T(8,128)(2,1)S(1)}, u32[]{:S(2)}, u32[]{:S(2)}) collective-permute-start(bf16[8,3,64,128]{3,2,1,0:T(8,128)(2,1)S(1)} %get-tuple-element.30), channel_id=1, source_target_pairs={{4,8},{8,4},{5,9},{9,5},{6,10},{10,6},{7,11},{11,7},{20,24},{24,20... | collective-permute-start | bytes 1179656 | tf_op jit(solution)/shard_map/ppermute | solution.py:31
  7.6 12.5 %collective-permute-start.2 = (bf16[3,8,64,128]{3,2,1,0:T(8,128)(2,1)S(1)}, bf16[3,8,64,128]{3,2,1,0:T(8,128)(2,1)S(1)}, u32[]{:S(2)}, u32[]{:S(2)}) collective-permute-start(bf16[3,8,64,128]{3,2,1,0:T(8,128)(2,1)S(1)} %get-tuple-element.32), channel_id=1, source_target_pairs={{0,1},{1,0},{2,3},{3,2},{4,5},{5,4},{6,7},{7,6},{8,9},{9,8},{10,11... | collective-permute-start | bytes 1179656 | tf_op jit(solution)/shard_map/ppermute | solution.py:31
  9.9 10.3 %collective-permute-start.3 = (bf16[3,8,64,128]{3,2,1,0:T(8,128)(2,1)S(1)}, bf16[3,8,64,128]{3,2,1,0:T(8,128)(2,1)S(1)}, u32[]{:S(2)}, u32[]{:S(2)}) collective-permute-start(bf16[3,8,64,128]{3,2,1,0:T(8,128)(2,1)S(1)} %get-tuple-element.33), channel_id=1, source_target_pairs={{1,2},{2,1},{5,6},{6,5},{9,10},{10,9},{13,14},{14,13},{17,18},{18,... | collective-permute-start | bytes 1179656 | tf_op jit(solution)/shard_map/ppermute | solution.py:31
  10.6 2.4 %collective-permute-start.6 = (bf16[3,3,64,128]{3,2,1,0:T(8,128)(2,1)S(1)}, bf16[3,3,64,128]{3,2,1,0:T(8,128)(2,1)S(1)}, u32[]{:S(2)}, u32[]{:S(2)}) collective-permute-start(bf16[3,3,64,128]{3,2,1,0:T(8,128)(2,1)S(1)} %get-tuple-element.36), channel_id=1, source_target_pairs={{5,10},{6,9},{9,6},{10,5},{21,26},{22,25},{25,22},{26,21}} | collective-permute-start | bytes 442376 | tf_op jit(solution)/shard_map/ppermute | solution.py:39
  15.8 8.6 %collective-permute-start.4 = (bf16[2,3,3,64,128]{4,3,2,1,0:T(8,128)(2,1)S(1)}, bf16[2,3,3,64,128]{4,3,2,1,0:T(8,128)(2,1)S(1)}, u32[]{:S(2)}, u32[]{:S(2)}) collective-permute-start(bf16[2,3,3,64,128]{4,3,2,1,0:T(8,128)(2,1)S(1)} %get-tuple-element.34), channel_id=1, source_target_pairs={{0,1},{1,0},{2,3},{3,2},{4,5},{5,4},{6,7},{7,6},{8,9},{9,8},{10,11... | collective-permute-start | bytes 884744 | tf_op jit(solution)/shard_map/ppermute | solution.py:31
  28.5 1.4 %collective-permute-start.7 = (f32[9,32,128]{2,1,0:T(8,128)S(1)}, f32[9,32,128]{2,1,0:T(8,128)S(1)}, u32[]{:S(2)}, u32[]{:S(2)}) collective-permute-start(f32[9,32,128]{2,1,0:T(8,128)S(1)} %get-tuple-element.48), channel_id=1, source_target_pairs={{0,1},{1,0},{2,3},{3,2},{4,5},{5,4},{6,7},{7,6},{8,9},{9,8},{10,11... | collective-permute-start | bytes 442376 | tf_op jit(solution)/shard_map/ppermute | solution.py:425
  30.0 4.6 %collective-permute-start.8 = (f32[9,16,128]{2,1,0:T(8,128)S(1)}, f32[9,16,128]{2,1,0:T(8,128)S(1)}, u32[]{:S(2)}, u32[]{:S(2)}) collective-permute-start(f32[9,16,128]{2,1,0:T(8,128)S(1)} %get-tuple-element.50), channel_id=1, source_target_pairs={{0,2},{1,3},{2,0},{3,1},{4,6},{5,7},{6,4},{7,5},{8,10},{9,11},{10,... | collective-permute-start | bytes 221192 | tf_op jit(solution)/shard_map/ppermute | solution.py:425

commit v4 on v3

--- a/solution.py
+++ b/solution.py
@@ -27,8 +27,11 @@
     return far_pairs(count) if far else near_pairs(count)
 
 
-def swap(block, axis, far):
-    return lax.ppermute(block, axis, partners(axis, far))
+def swap(block, axis, far, name):
+    pairs = partners(axis, far)
+    if name == "tile_far":
+        pairs = pairs + [(i, i) for i in sorted({0, lax.axis_size(axis) - 1})]
+    return lax.ppermute(block, axis, pairs)
 
 
 def swap_corner(block, far):
@@ -80,6 +83,12 @@
     for i, ref in enumerate((near_ref, far_ref)):
         given_ref[i] = ref[pl.ds(start, HALO)]
         both_ref[i] = ref[...]
+    index = lax.axis_index("tile")
+
+    @pl.when((index == 0) | (index == lax.axis_size("tile") - 1))
+    def _():
+        both_ref[1] = jnp.zeros(both_ref.shape[1:], BF16)
+        given_ref[1] = jnp.zeros(given_ref.shape[1:], BF16)
 
 
 def shifted_sum(parts, spacing, chans):
@@ -382,13 +391,13 @@
             jax.ShapeDtypeStruct((2, planes, HALO, chans, lanes), BF16),
             jax.ShapeDtypeStruct((2, HALO, HALO, chans, lanes), BF16),
         ),
-        (swap(tn, "tile", False), swap(tf, "tile", True)),
+        (swap(tn, "tile", False, "tile_near"), swap(tf, "tile", True, "tile_far")),
         1 << 20,
         4,
     )
     far_corners = jnp.stack([swap_corner(cn, False), swap_corner(cf, True)])
-    depths = jnp.stack([swap(dn, "depth", False), swap(df, "depth", True)])
-    corners = jnp.stack([swap(given, "depth", False), far_corners])
+    depths = jnp.stack([swap(dn, "depth", False, "depth_near"), swap(df, "depth", True, "depth_far")])
+    corners = jnp.stack([swap(given, "depth", False, "forward"), far_corners])
 
     row_flops = 2 * 27 * chans * chans * lanes
     hidden_shape = jax.ShapeDtypeStruct((planes + 4, rows + 4, chans, lanes), BF16)

time: 35.5 us -> 35.5 us (level)
  no operation moved by 1% of the time
where the time goes in v4:
time: 35.5 us; the launch traced here: 35.3 us
  starting transfers between devices  15.3 us (43%)
  Pallas kernels  12.5 us (35%)
  waiting for transfers between devices  7.08 us (20%)
    pallas_call x8, Pallas kernels, call(): pl.pallas_call(kernel, out_shape=outs, in_specs=[pl.BlockSpec(memory_spac...  12.5 us
    ppermute x5, starting transfers between devices, swap(): return lax.ppermute(block, axis, pairs)  12.4 us
    ppermute x2, waiting for transfers between devices, body(): lax.ppermute(send, 'depth', [(i, i ^ 1 << level) for i in range(count)])  4.44 us
    ppermute x5, waiting for transfers between devices, swap(): return lax.ppermute(block, axis, pairs)  2.63 us
    ppermute x2, starting transfers between devices, body(): lax.ppermute(send, 'depth', [(i, i ^ 1 << level) for i in range(count)])  1.56 us
    ppermute x2, starting transfers between devices, swap_corner(): return lax.ppermute(block, ('tile', 'depth'), pairs)  1.34 us
  transfers between devices with their start and end apart: 9, of which 3 were waited for; matrix products, arithmetic and copies ran while one was open for 0% of the time, Pallas kernels for 17%

profile of v4, /device:TPU:12, one launch (start us, length us, event | category | flops | bytes accessed | tf_op | source)
XLA Modules:
  0.0 35.3 jit_solution(11861495458274822766)
XLA Ops:
  0.0 1.8 %shard_map.64 = (bf16[8,8,64,128]{3,2,1,0:T(8,128)(2,1)S(1)}, bf16[8,3,64,128]{3,2,1,0:T(8,128)(2,1)S(1)}, bf16[8,3,64,128]{3,2,1,0:T(8,128)(2,1)S(1)}, bf16[3,8...) custom-call(bf16[64,8,8,128]{3,2,1,0:T(8,128)(2,1)} %volume_ref.1, ...), custom_call_target="tpu_custom_call" | custom-call | flops 1048576 | bytes 1048576 | tf_op jit(solution)/shard_map/pallas_call | solution.py:349
  1.8 0.7 %collective-permute-start.5 = (bf16[3,3,64,128]{3,2,1,0:T(8,128)(2,1)S(1)}, bf16[3,3,64,128]{3,2,1,0:T(8,128)(2,1)S(1)}, u32[]{:S(2)}, u32[]{:S(2)}) collective-permute-start(bf16[3,3,64,128]{3,2,1,0:T(8,128)(2,1)S(1)} %get-tuple-element.35), channel_id=1, source_target_pairs={{1,6},{2,5},{5,2},{6,1},{9,14},{10,13},{13,10},{14,9},{17,22},{18,... | collective-permute-start | bytes 442376 | tf_op jit(solution)/shard_map/ppermute | solution.py:42
  2.5 0.5 %collective-permute-start = (bf16[8,3,64,128]{3,2,1,0:T(8,128)(2,1)S(1)}, bf16[8,3,64,128]{3,2,1,0:T(8,128)(2,1)S(1)}, u32[]{:S(2)}, u32[]{:S(2)}) collective-permute-start(bf16[8,3,64,128]{3,2,1,0:T(8,128)(2,1)S(1)} %get-tuple-element.29), channel_id=1, source_target_pairs={{0,4},{4,0},{8,12},{12,8},{1,5},{5,1},{9,13},{13,9},{2,6},{6,2},{1... | collective-permute-start | bytes 1179656 | tf_op jit(solution)/shard_map/ppermute | solution.py:34
  3.0 4.6 %collective-permute-start.1 = (bf16[8,3,64,128]{3,2,1,0:T(8,128)(2,1)S(1)}, bf16[8,3,64,128]{3,2,1,0:T(8,128)(2,1)S(1)}, u32[]{:S(2)}, u32[]{:S(2)}) collective-permute-start(bf16[8,3,64,128]{3,2,1,0:T(8,128)(2,1)S(1)} %get-tuple-element.30), channel_id=1, source_target_pairs={{4,8},{8,4},{0,0},{12,12},{5,9},{9,5},{1,1},{13,13},{6,10},{10,6},... | collective-permute-start | bytes 1179656 | tf_op jit(solution)/shard_map/ppermute | solution.py:34
  7.6 2.2 %collective-permute-start.2 = (bf16[3,8,64,128]{3,2,1,0:T(8,128)(2,1)S(1)}, bf16[3,8,64,128]{3,2,1,0:T(8,128)(2,1)S(1)}, u32[]{:S(2)}, u32[]{:S(2)}) collective-permute-start(bf16[3,8,64,128]{3,2,1,0:T(8,128)(2,1)S(1)} %get-tuple-element.32), channel_id=1, source_target_pairs={{0,1},{1,0},{2,3},{3,2},{4,5},{5,4},{6,7},{7,6},{8,9},{9,8},{10,11... | collective-permute-start | bytes 1179656 | tf_op jit(solution)/shard_map/ppermute | solution.py:34
  9.9 0.7 %collective-permute-start.3 = (bf16[3,8,64,128]{3,2,1,0:T(8,128)(2,1)S(1)}, bf16[3,8,64,128]{3,2,1,0:T(8,128)(2,1)S(1)}, u32[]{:S(2)}, u32[]{:S(2)}) collective-permute-start(bf16[3,8,64,128]{3,2,1,0:T(8,128)(2,1)S(1)} %get-tuple-element.33), channel_id=1, source_target_pairs={{1,2},{2,1},{5,6},{6,5},{9,10},{10,9},{13,14},{14,13},{17,18},{18,... | collective-permute-start | bytes 1179656 | tf_op jit(solution)/shard_map/ppermute | solution.py:34
  10.6 0.0 collective-permute-done.5
  10.6 0.7 %collective-permute-start.6 = (bf16[3,3,64,128]{3,2,1,0:T(8,128)(2,1)S(1)}, bf16[3,3,64,128]{3,2,1,0:T(8,128)(2,1)S(1)}, u32[]{:S(2)}, u32[]{:S(2)}) collective-permute-start(bf16[3,3,64,128]{3,2,1,0:T(8,128)(2,1)S(1)} %get-tuple-element.36), channel_id=1, source_target_pairs={{5,10},{6,9},{9,6},{10,5},{21,26},{22,25},{25,22},{26,21}} | collective-permute-start | bytes 442376 | tf_op jit(solution)/shard_map/ppermute | solution.py:42
  11.2 1.7 %shard_map.66 = (bf16[12,12,64,128]{3,2,1,0:T(8,128)(2,1)S(1)}, bf16[192,576]{1,0:T(8,128)(2,1)S(1)}, bf16[192,576]{1,0:T(8,128)(2,1)S(1)}) custom-call(bf16[8,8,64,128]{3,2,1,0:T(8,128)(2,1)S(1)} %get-tuple-element.28.own_ref, bf16[27,64,64]{2,1,0:T(8,128)(2,1)S(1)} %get-tuple-element.37.w1_ref, f32[1,64]{1,0:T(1,128)S(1)} %get-tuple-element.38.b1_ref, ...), custom_call_target="tpu_custom_call" | custom-call | flops 1019215872 | bytes 1048576 | tf_op jit(solution)/shard_map/pallas_call | solution.py:349
  13.0 0.0 collective-permute-done.6
  13.0 0.0 collective-permute-done.near_ref
  13.1 2.6 %collective-permute-done.1.far_ref = bf16[8,3,64,128]{3,2,1,0:T(8,128)(2,1)S(1)} collective-permute-done((bf16[8,3,64,128]{3,2,1,0:T(8,128)(2,1)S(1)}, bf16[8,3,64,128]{3,2,1,0:T(8,128)(2,1)S(1)}, u32[]{:S(2)}, u32[]{:S(2)}) %collective-permute-start.1) | collective-permute-done | bytes 393248 | tf_op jit(solution)/shard_map/ppermute | solution.py:34
  15.7 0.1 shard_map.65
  15.8 4.4 %collective-permute-start.4 = (bf16[2,3,3,64,128]{4,3,2,1,0:T(8,128)(2,1)S(1)}, bf16[2,3,3,64,128]{4,3,2,1,0:T(8,128)(2,1)S(1)}, u32[]{:S(2)}, u32[]{:S(2)}) collective-permute-start(bf16[2,3,3,64,128]{4,3,2,1,0:T(8,128)(2,1)S(1)} %get-tuple-element.34), channel_id=1, source_target_pairs={{0,1},{1,0},{2,3},{3,2},{4,5},{5,4},{6,7},{7,6},{8,9},{9,8},{10,11... | collective-permute-start | bytes 884744 | tf_op jit(solution)/shard_map/ppermute | solution.py:34
  20.2 0.0 collective-permute-done.2
  20.2 0.0 collective-permute-done.3
  20.2 0.1 pad_maximum_fusion.halo_ref.depths_ref
  20.3 1.7 %shard_map.67.given_ref = bf16[12,12,64,128]{3,2,1,0:T(8,128)(2,1)S(1)} custom-call(bf16[8,8,64,128]{3,2,1,0:T(8,128)(2,1)S(1)} %get-tuple-element.28.own_ref, bf16[2,3,8,64,128]{4,3,2,1,0:T(8,128)(2,1)S(1)} %pad_maximum_fusion.halo_ref.depths_ref, bf16[192,576]{1,0:T(8,128)(2,1)S(1)} %get-tuple-element.40.taps_ref.taps1_ref, ...), custom_call_target="tpu_custom_call", output_to_operand_aliasing={{}: (4, {})} | custom-call | flops 1019215872 | bytes 1048576 | tf_op jit(solution)/shard_map/pallas_call | solution.py:349
  22.0 2.4 %shard_map.68 = (bf16[12,12,64,128]{3,2,1,0:T(8,128)(2,1)S(1)}, f32[2,72,128]{2,1,0:T(8,128)S(1)}) custom-call(bf16[8,8,64,128]{3,2,1,0:T(8,128)(2,1)S(1)} %get-tuple-element.28.own_ref, bf16[2,8,3,64,128]{4,3,2,1,0:T(8,128)(2,1)S(1)} %get-tuple-element.31.halo_ref.tiles_ref, ...), custom_call_target="tpu_custom_call", output_to_operand_aliasing={{0}: (7, {})} | custom-call | flops 1472200704 | bytes 1048576 | tf_op jit(solution)/shard_map/pallas_call | solution.py:349
  24.4 0.0 collective-permute-done.4
  24.4 0.1 pad_maximum_fusion.1.corners_ref
  24.4 4.1 %shard_map.69 = (bf16[12,12,64,128]{3,2,1,0:T(8,128)(2,1)S(1)}, f32[9,32,128]{2,1,0:T(8,128)S(1)}, f32[9,32,128]{2,1,0:T(8,128)S(1)}) custom-call(bf16[8,8,64,128]{3,2,1,0:T(8,128)(2,1)S(1)} %get-tuple-element.28.own_ref, bf16[2,8,3,64,128]{4,3,2,1,0:T(8,128)(2,1)S(1)} %get-tuple-element.31.halo_ref.tiles_ref, ...), custom_call_target="tpu_custom_call", output_to_operand_aliasing={{0}: (9, {})} | custom-call | flops 2378170368 | bytes 1048576 | tf_op jit(solution)/shard_map/pallas_call | solution.py:349
  28.5 0.4 %collective-permute-start.7 = (f32[9,32,128]{2,1,0:T(8,128)S(1)}, f32[9,32,128]{2,1,0:T(8,128)S(1)}, u32[]{:S(2)}, u32[]{:S(2)}) collective-permute-start(f32[9,32,128]{2,1,0:T(8,128)S(1)} %get-tuple-element.48), channel_id=1, source_target_pairs={{0,1},{1,0},{2,3},{3,2},{4,5},{5,4},{6,7},{7,6},{8,9},{9,8},{10,11... | collective-permute-start | bytes 442376 | tf_op jit(solution)/shard_map/ppermute | solution.py:434
  28.9 1.0 %collective-permute-done.7.other_ref = f32[9,32,128]{2,1,0:T(8,128)S(1)} collective-permute-done((f32[9,32,128]{2,1,0:T(8,128)S(1)}, f32[9,32,128]{2,1,0:T(8,128)S(1)}, u32[]{:S(2)}, u32[]{:S(2)}) %collective-permute-start.7) | collective-permute-done | bytes 147488 | tf_op jit(solution)/shard_map/ppermute | solution.py:434
  30.0 1.2 %collective-permute-start.8 = (f32[9,16,128]{2,1,0:T(8,128)S(1)}, f32[9,16,128]{2,1,0:T(8,128)S(1)}, u32[]{:S(2)}, u32[]{:S(2)}) collective-permute-start(f32[9,16,128]{2,1,0:T(8,128)S(1)} %get-tuple-element.50), channel_id=1, source_target_pairs={{0,2},{1,3},{2,0},{3,1},{4,6},{5,7},{6,4},{7,5},{8,10},{9,11},{10,... | collective-permute-start | bytes 221192 | tf_op jit(solution)/shard_map/ppermute | solution.py:434
  31.2 3.4 %collective-permute-done.8.other_ref = f32[9,16,128]{2,1,0:T(8,128)S(1)} collective-permute-done((f32[9,16,128]{2,1,0:T(8,128)S(1)}, f32[9,16,128]{2,1,0:T(8,128)S(1)}, u32[]{:S(2)}, u32[]{:S(2)}) %collective-permute-start.8) | collective-permute-done | bytes 73760 | tf_op jit(solution)/shard_map/ppermute | solution.py:434
  34.6 0.7 %shard_map.71 = f32[16,8,128]{2,1,0:T(8,128)} custom-call(f32[9,16,128]{2,1,0:T(8,128)S(1)} %get-tuple-element.49.mine_ref, f32[9,16,128]{2,1,0:T(8,128)S(1)} %collective-permute-done.8.other_ref), custom_call_target="tpu_custom_call" | custom-call | flops 1048576 | bytes 1048576 | tf_op jit(solution)/shard_map/pallas_call | solution.py:349
  (2 shorter events, 0.1 us)
Async XLA Ops:
  1.8 8.7 %collective-permute-start.5 = (bf16[3,3,64,128]{3,2,1,0:T(8,128)(2,1)S(1)}, bf16[3,3,64,128]{3,2,1,0:T(8,128)(2,1)S(1)}, u32[]{:S(2)}, u32[]{:S(2)}) collective-permute-start(bf16[3,3,64,128]{3,2,1,0:T(8,128)(2,1)S(1)} %get-tuple-element.35), channel_id=1, source_target_pairs={{1,6},{2,5},{5,2},{6,1},{9,14},{10,13},{13,10},{14,9},{17,22},{18,... | collective-permute-start | bytes 442376 | tf_op jit(solution)/shard_map/ppermute | solution.py:42
  2.5 10.6 %collective-permute-start = (bf16[8,3,64,128]{3,2,1,0:T(8,128)(2,1)S(1)}, bf16[8,3,64,128]{3,2,1,0:T(8,128)(2,1)S(1)}, u32[]{:S(2)}, u32[]{:S(2)}) collective-permute-start(bf16[8,3,64,128]{3,2,1,0:T(8,128)(2,1)S(1)} %get-tuple-element.29), channel_id=1, source_target_pairs={{0,4},{4,0},{8,12},{12,8},{1,5},{5,1},{9,13},{13,9},{2,6},{6,2},{1... | collective-permute-start | bytes 1179656 | tf_op jit(solution)/shard_map/ppermute | solution.py:34
  3.0 12.6 %collective-permute-start.1 = (bf16[8,3,64,128]{3,2,1,0:T(8,128)(2,1)S(1)}, bf16[8,3,64,128]{3,2,1,0:T(8,128)(2,1)S(1)}, u32[]{:S(2)}, u32[]{:S(2)}) collective-permute-start(bf16[8,3,64,128]{3,2,1,0:T(8,128)(2,1)S(1)} %get-tuple-element.30), channel_id=1, source_target_pairs={{4,8},{8,4},{0,0},{12,12},{5,9},{9,5},{1,1},{13,13},{6,10},{10,6},... | collective-permute-start | bytes 1179656 | tf_op jit(solution)/shard_map/ppermute | solution.py:34
  7.6 12.5 %collective-permute-start.2 = (bf16[3,8,64,128]{3,2,1,0:T(8,128)(2,1)S(1)}, bf16[3,8,64,128]{3,2,1,0:T(8,128)(2,1)S(1)}, u32[]{:S(2)}, u32[]{:S(2)}) collective-permute-start(bf16[3,8,64,128]{3,2,1,0:T(8,128)(2,1)S(1)} %get-tuple-element.32), channel_id=1, source_target_pairs={{0,1},{1,0},{2,3},{3,2},{4,5},{5,4},{6,7},{7,6},{8,9},{9,8},{10,11... | collective-permute-start | bytes 1179656 | tf_op jit(solution)/shard_map/ppermute | solution.py:34
  9.9 10.3 %collective-permute-start.3 = (bf16[3,8,64,128]{3,2,1,0:T(8,128)(2,1)S(1)}, bf16[3,8,64,128]{3,2,1,0:T(8,128)(2,1)S(1)}, u32[]{:S(2)}, u32[]{:S(2)}) collective-permute-start(bf16[3,8,64,128]{3,2,1,0:T(8,128)(2,1)S(1)} %get-tuple-element.33), channel_id=1, source_target_pairs={{1,2},{2,1},{5,6},{6,5},{9,10},{10,9},{13,14},{14,13},{17,18},{18,... | collective-permute-start | bytes 1179656 | tf_op jit(solution)/shard_map/ppermute | solution.py:34
  10.6 2.4 %collective-permute-start.6 = (bf16[3,3,64,128]{3,2,1,0:T(8,128)(2,1)S(1)}, bf16[3,3,64,128]{3,2,1,0:T(8,128)(2,1)S(1)}, u32[]{:S(2)}, u32[]{:S(2)}) collective-permute-start(bf16[3,3,64,128]{3,2,1,0:T(8,128)(2,1)S(1)} %get-tuple-element.36), channel_id=1, source_target_pairs={{5,10},{6,9},{9,6},{10,5},{21,26},{22,25},{25,22},{26,21}} | collective-permute-start | bytes 442376 | tf_op jit(solution)/shard_map/ppermute | solution.py:42
  15.8 8.6 %collective-permute-start.4 = (bf16[2,3,3,64,128]{4,3,2,1,0:T(8,128)(2,1)S(1)}, bf16[2,3,3,64,128]{4,3,2,1,0:T(8,128)(2,1)S(1)}, u32[]{:S(2)}, u32[]{:S(2)}) collective-permute-start(bf16[2,3,3,64,128]{4,3,2,1,0:T(8,128)(2,1)S(1)} %get-tuple-element.34), channel_id=1, source_target_pairs={{0,1},{1,0},{2,3},{3,2},{4,5},{5,4},{6,7},{7,6},{8,9},{9,8},{10,11... | collective-permute-start | bytes 884744 | tf_op jit(solution)/shard_map/ppermute | solution.py:34
  28.5 1.4 %collective-permute-start.7 = (f32[9,32,128]{2,1,0:T(8,128)S(1)}, f32[9,32,128]{2,1,0:T(8,128)S(1)}, u32[]{:S(2)}, u32[]{:S(2)}) collective-permute-start(f32[9,32,128]{2,1,0:T(8,128)S(1)} %get-tuple-element.48), channel_id=1, source_target_pairs={{0,1},{1,0},{2,3},{3,2},{4,5},{5,4},{6,7},{7,6},{8,9},{9,8},{10,11... | collective-permute-start | bytes 442376 | tf_op jit(solution)/shard_map/ppermute | solution.py:434
  30.0 4.6 %collective-permute-start.8 = (f32[9,16,128]{2,1,0:T(8,128)S(1)}, f32[9,16,128]{2,1,0:T(8,128)S(1)}, u32[]{:S(2)}, u32[]{:S(2)}) collective-permute-start(f32[9,16,128]{2,1,0:T(8,128)S(1)} %get-tuple-element.50), channel_id=1, source_target_pairs={{0,2},{1,3},{2,0},{3,1},{4,6},{5,7},{6,4},{7,5},{8,10},{9,11},{10,... | collective-permute-start | bytes 221192 | tf_op jit(solution)/shard_map/ppermute | solution.py:434
